TPU v7x, 32 devices: a whole 2x2x4 slice. The times are simulated.
32 devices in a mesh: scene: 2 (over y), tok: 4 (over z), col: 2 (over x), rep: 2 (over core).
Axes of the slice: x: 2, y: 2, z: 4, core: 2. Of those that a mesh axis runs over, the one named last changes fastest.
Arguments:
- tokens: float32 [8192, 512], P(('scene', 'tok'), ('col', 'rep')), parts along dimension 0
- w_qkv: float32 [2, 3, 512, 512], P(None, None, None, ('col', 'rep'))
- w_out: float32 [2, 512, 512], P(None, ('col', 'rep')), may hold values from -0.25 to 0.25
- w_up: float32 [2, 512, 2048], P(None, None, ('col', 'rep')), may hold values from -0.25 to 0.25
- w_down: float32 [2, 2048, 512], P(None, ('col', 'rep')), may hold values from -0.125 to 0.125
- attn_gain: float32 [2, 512], replicated, may hold values from 0.1 to 1.9
- mlp_gain: float32 [2, 512], replicated, may hold values from 0.1 to 1.9
- dest_device: int32 [128], P(('scene', 'tok')), parts along dimension 0, may hold values from 0 to 3, as said below
- dest_slot: int32 [128], P(('scene', 'tok')), parts along dimension 0, may hold values from 0 to 15, as said below
- pillar: int32 [8192], P(('scene', 'tok')), parts along dimension 0, may hold values from -1 to 2047, as said below
- depth_weight: float32 [2, 3, 3, 512], replicated, may hold values from -2 to 2
- point_weight: float32 [2, 512, 1024], replicated, may hold values from -0.25 to 0.25
- raster_gain: float32 [2, 512], replicated, may hold values from 0.1 to 1.9
Outputs:
- raster: float32 [128, 32, 512], P(('scene', 'tok', 'rep'), 'col'), parts along dimension 0
There are 2 independent parts, one for each index of `scene`. A program takes and returns all parts, laid end to end along the dimension named above; an argument that names none is the same for every part. Nothing has to cross between parts.
Inputs may be any that keep to these rules, and one draw needn't show every extreme that they name: `dest_device`: together with dest_slot the blocks fill every index of tok's 16 slots exactly once. At most 5 blocks of one index of tok go to one index, and every index sends exactly 5 blocks to some index. `dest_slot`: the slot of the block among the 16 of its destination. The token at Hilbert position t has a cell in raster rows i * 16 to (i + 1) * 16 - 1 with i = t // 1024, or -1 if it has no pillar; several tokens may share a cell.
All inputs are finite; a program needn't handle non-finite values.
Results may differ from a plain program's by a relative error of at most 0.00012.
Values sent between devices are 32-bit elements; how exact they have to be, the bound alone decides.
A program may use at most 128 MiB of HBM per device.

v0:
```python
import functools
import math

import jax
import jax.numpy as jnp
from jax import lax
from jax.experimental import pallas as pl
from jax.experimental.pallas import tpu as pltpu
from jax.sharding import PartitionSpec as P

PATCH = 1024
TR = 16
TC = 16
HD = 16


MATMUL_PRECISION = lax.Precision.HIGH
EPSILON = 1e-05


def layer_norm(values, gain_row):
    average = jnp.mean(values, axis=-1, keepdims=True)
    centered = values - average
    variance = jnp.mean(centered * centered, axis=-1, keepdims=True)
    return centered * lax.rsqrt(variance + EPSILON) * gain_row


def split(values):
    high = values.astype(jnp.bfloat16)
    return high, (values - high.astype(jnp.float32)).astype(jnp.bfloat16)


def bdot(left, right, dims=(((1,), (0,)), ((), ()))):
    return lax.dot_general(left, right, dims, preferred_element_type=jnp.float32)


def dot3(left, right):
    lh, ll = left
    rh, rl = right
    return bdot(lh, rh) + bdot(lh, rl) + bdot(ll, rh)


def attention_kernel(share, source_ref, x_ref, gain_ref, w_ref, o_ref, out_ref, q_s, k_s, v_s, att_s):
    cols = w_ref.shape[-1]
    heads = cols // HD
    rows = out_ref.shape[0]
    chunk = att_s.shape[0]
    slots, each, block = x_ref.shape[1:4]
    first_block = pl.program_id(0) * (rows // block)

    def stream_rows(i):
        parts = []
        for n in range(chunk // block):
            at = source_ref[first_block + i * (chunk // block) + n]
            places = [x_ref[at // each, j, at % each] for j in range(slots)]
            parts.append(jnp.concatenate(places, axis=-1))
        return jnp.concatenate(parts, axis=0)

    lanes = q_s.shape[-1]

    r = lax.broadcasted_iota(jnp.int32, (cols, lanes), 0)
    c = lax.broadcasted_iota(jnp.int32, (cols, lanes), 1)
    lane = lax.broadcasted_iota(jnp.int32, (1, cols), 1)
    w = [split(w_ref[j]) for j in range(3)]
    for i in range(rows // chunk):
        at = pl.ds(i * chunk, chunk)
        normed = split(layer_norm(stream_rows(i), gain_ref[...]))
        qh, ql = split(dot3(normed, w[0]) * (HD ** (-0.5) * math.log2(math.e)))
        kh, kl = split(dot3(normed, w[1]))
        vh, vl = split(dot3(normed, w[2]))
        for h in range(heads):
            part = c // HD
            inside = (r // HD == h) & (r % HD == c % HD)
            first = (inside & ((part == 0) | (part == 1))).astype(jnp.bfloat16)
            third = (inside & (part == 2)).astype(jnp.bfloat16)
            outer = (inside & ((part == 0) | (part == 2))).astype(jnp.bfloat16)
            middle = (inside & (part == 1)).astype(jnp.bfloat16)
            q_s[h, at, :] = (bdot(qh, first) + bdot(ql, third)).astype(jnp.bfloat16)
            k_s[h, at, :] = (bdot(kh, outer) + bdot(kl, middle)).astype(jnp.bfloat16)
            own = lane // HD == h
            v_s[h, at, :cols] = jnp.where(own, vh.astype(jnp.float32), 0.0).astype(jnp.bfloat16)
            v_s[h, at, cols:] = jnp.where(own, vl.astype(jnp.float32), 1.0).astype(jnp.bfloat16)

    projection = split(o_ref[...])

    def query_rows(i, carry):
        at = pl.ds(pl.multiple_of(i * chunk, chunk), chunk)
        att_s[...] = jnp.zeros_like(att_s)

        def one_head(h, carry):
            scores = bdot(q_s[h, at, :], k_s[h], (((1,), (1,)), ((), ())))
            weights = jnp.exp2(scores - jnp.max(scores, axis=-1, keepdims=True))
            wh, wl = split(weights)
            sums = bdot(wh, v_s[h]) + bdot(wl, v_s[h])
            top, low = sums[:, :cols], sums[:, cols:]
            own = lane // HD == h
            total = jnp.max(jnp.where(own, 0.0, low), axis=-1, keepdims=True)
            att_s[...] += jnp.where(own, (top + low) / total, 0.0)
            return carry

        lax.fori_loop(0, heads, one_head, 0, unroll=4)
        out_ref[at, :] = dot3(split(att_s[...]), projection) + stream_rows(i) * share
        return carry

    lax.fori_loop(0, rows // chunk, query_rows, 0)


def attend(blocks, source, gain_row, weights, w_out, group):
    block, width = blocks.shape[3], blocks.shape[1] * blocks.shape[4]
    rows = source.shape[0] * block
    cols = weights.shape[-1]
    heads = cols // HD
    lanes = max(128, 3 * HD)
    return pl.pallas_call(
        functools.partial(attention_kernel, 1.0 / group),
        grid_spec=pltpu.PrefetchScalarGridSpec(
            num_scalar_prefetch=1,
            grid=(rows // PATCH,),
            in_specs=[
                pl.BlockSpec(blocks.shape, lambda i, source: (0, 0, 0, 0, 0)),
                pl.BlockSpec((1, width), lambda i, source: (0, 0)),
                pl.BlockSpec(weights.shape, lambda i, source: (0, 0, 0)),
                pl.BlockSpec(w_out.shape, lambda i, source: (0, 0)),
            ],
            out_specs=pl.BlockSpec((PATCH, width), lambda i, source: (i, 0)),
            scratch_shapes=[
                pltpu.VMEM((heads, PATCH, lanes), jnp.bfloat16),
                pltpu.VMEM((heads, PATCH, lanes), jnp.bfloat16),
                pltpu.VMEM((heads, PATCH, 2 * cols), jnp.bfloat16),
                pltpu.VMEM((256, cols), jnp.float32),
            ],
        ),
        out_shape=jax.ShapeDtypeStruct((rows, width), jnp.float32),
        compiler_params=pltpu.CompilerParams(vmem_limit_bytes=48 * 1024 * 1024),
        name="attend",
    )(source, blocks, gain_row[None, :], weights, w_out)


def matmul(left, right):
    return jnp.dot(left, right, precision=MATMUL_PRECISION, preferred_element_type=jnp.float32)


VMEM_LIMIT = 56 * 1024 * 1024
MESH = pl.DeviceIdType.MESH


def position():
    cols, reps = lax.axis_size("col"), lax.axis_size("rep")
    return cols, reps, lax.axis_index("col"), lax.axis_index("rep")


def greet(devices):
    barrier = pltpu.get_barrier_semaphore()
    for device in devices:
        pl.semaphore_signal(barrier, inc=1, device_id=device, device_id_type=MESH)
    pl.semaphore_wait(barrier, len(devices))


def remote(src, dst, send, recv, device):
    return pltpu.make_async_remote_copy(
        src_ref=src, dst_ref=dst, send_sem=send, recv_sem=recv, device_id=device, device_id_type=MESH
    )


def chunks_of(rows):
    for pieces in (8, 5, 4, 2):
        if rows % (8 * pieces) == 0:
            return pieces, rows // pieces
    return 1, rows


def gather_kernel(x_ref, out_ref, xs, xr, fs, fr, ps, pr, local):
    cols, reps, c, r = position()
    rows = x_ref.shape[0]
    pieces, size = chunks_of(rows)
    me = c * reps + r
    mate = {"col": c, "rep": 1 - r}
    others = [{"col": lax.rem(c + d, cols), "rep": r} for d in range(1, cols)]
    greet([mate] + others)
    across, onward = [], []
    for k in range(pieces):
        at = pl.ds(k * size, size)
        for d in range(1, cols):
            copy = remote(
                x_ref.at[at], out_ref.at[me, at], xs.at[d - 1, k], xr.at[d - 1, k], others[d - 1]
            )
            copy.start()
            across.append(copy)
    share = remote(x_ref, out_ref.at[me], ps, pr, mate)
    share.start()
    keep = pltpu.make_async_copy(x_ref, out_ref.at[me], local)
    keep.start()
    for k in range(pieces):
        at = pl.ds(k * size, size)
        for d in range(1, cols):
            across[k * (cols - 1) + d - 1].wait_recv()
            slot = lax.rem(c + cols - d, cols) * reps + r
            copy = remote(
                out_ref.at[slot, at], out_ref.at[slot, at], fs.at[d - 1, k], fr.at[d - 1, k], mate
            )
            copy.start()
            onward.append(copy)
    for copy in across:
        copy.wait_send()
    share.wait()
    keep.wait()
    for copy in onward:
        copy.wait()


def gather(block, collective_id):
    cols, reps = lax.axis_size("col"), lax.axis_size("rep")
    if reps != 2 or cols < 2:
        return lax.all_gather(block, ("col", "rep"), axis=0)
    pieces, _ = chunks_of(block.shape[0])
    dma = pltpu.SemaphoreType.DMA
    return pl.pallas_call(
        gather_kernel,
        out_shape=jax.ShapeDtypeStruct((cols * reps,) + block.shape, block.dtype),
        in_specs=[pl.BlockSpec(memory_space=pltpu.VMEM)],
        out_specs=pl.BlockSpec(memory_space=pltpu.VMEM),
        scratch_shapes=[dma((cols - 1, pieces))] * 4 + [dma, dma, dma],
        compiler_params=pltpu.CompilerParams(
            collective_id=collective_id, has_side_effects=True, vmem_limit_bytes=VMEM_LIMIT
        ),
        name="gather",
    )(block)


def scatter_kernel(edge, p_ref, out_ref, a_ref, s_ref, b_ref, a_s, a_r, b_s, b_r, *halo):
    cols, reps, c, r = position()
    rows = p_ref.shape[1]
    pieces, size = chunks_of(rows)
    mate = {"col": c, "rep": 1 - r}
    others = [{"col": lax.rem(c + d, cols), "rep": r} for d in range(1, cols)]
    greeted = [mate] + others
    if edge:
        ntok, t = lax.axis_size("tok"), lax.axis_index("tok")
        partner = {"tok": lax.rem(t + jnp.where(r == 0, ntok - 1, 1), ntok), "rep": 1 - r}
        greeted = greeted + [partner]
    greet(greeted)
    order = [(k, d) for k in range(pieces) for d in range(1, cols)]
    order += [(k, 0) for k in range(pieces)]
    near, far = {}, {}
    for k, d in order:
        at = pl.ds(k * size, size)
        slot = lax.rem(c + d, cols) * reps + 1 - r
        near[k, d] = remote(
            p_ref.at[slot, at], a_ref.at[d, at], a_s.at[d, k], a_r.at[d, k], mate
        )
        near[k, d].start()
    for k, d in order:
        at = pl.ds(k * size, size)
        slot = lax.rem(c + d, cols) * reps + r
        near[k, d].wait_recv()
        total = p_ref[slot, at] + a_ref[d, at]
        if d == 0:
            out_ref[at] = total
        else:
            s_ref[d - 1, at] = total
            far[k, d] = remote(
                s_ref.at[d - 1, at],
                b_ref.at[d - 1, at],
                b_s.at[d - 1, k],
                b_r.at[d - 1, k],
                others[d - 1],
            )
            far[k, d].start()
    for (k, d), copy in far.items():
        at = pl.ds(k * size, size)
        copy.wait_recv()
        out_ref[at] += b_ref[d - 1, at]
    if edge:
        h_ref, e_ref, h_s, h_r = halo
        inner = pl.multiple_of(jnp.where(r == 0, edge, rows - 2 * edge), 8)
        outer = pl.multiple_of(jnp.where(r == 0, 0, rows - edge), 8)
        e_ref[...] = out_ref[pl.ds(inner, edge)]
        copy = remote(e_ref, h_ref, h_s, h_r, partner)
        copy.start()
        copy.wait()
        wrapped = jnp.where(r == 0, t == 0, t == ntok - 1)
        out_ref[pl.ds(outer, edge)] = jnp.where(wrapped, 0.0, h_ref[...])
    for copy in list(near.values()) + list(far.values()):
        copy.wait_send()


def scatter(parts, collective_id, edge=0):
    cols, reps = lax.axis_size("col"), lax.axis_size("rep")
    if reps != 2 or cols < 2:
        return lax.psum_scatter(parts, ("col", "rep"), scatter_dimension=0)
    shape, kind = parts.shape[1:], parts.dtype
    pieces, _ = chunks_of(shape[0])
    dma = pltpu.SemaphoreType.DMA
    return pl.pallas_call(
        functools.partial(scatter_kernel, edge),
        out_shape=jax.ShapeDtypeStruct(shape, kind),
        in_specs=[pl.BlockSpec(memory_space=pltpu.VMEM)],
        out_specs=pl.BlockSpec(memory_space=pltpu.VMEM),
        scratch_shapes=[
            pltpu.VMEM((cols,) + shape, kind),
            pltpu.VMEM((cols - 1,) + shape, kind),
            pltpu.VMEM((cols - 1,) + shape, kind),
            dma((cols, pieces)),
            dma((cols, pieces)),
            dma((cols - 1, pieces)),
            dma((cols - 1, pieces)),
        ]
        + ([pltpu.VMEM((edge, shape[1]), kind)] * 2 + [dma, dma] if edge else []),
        compiler_params=pltpu.CompilerParams(
            collective_id=collective_id, has_side_effects=True, vmem_limit_bytes=VMEM_LIMIT
        ),
        name="scatter",
    )(parts)


def total_kernel(
    p_ref, out_ref, a_ref, s_ref, b_ref, a_s, a_r, b_s, b_r, xs, xr, fs, fr, ps, pr
):
    cols, reps, c, r = position()
    rows = p_ref.shape[1]
    pieces, size = chunks_of(rows)
    me = c * reps + r
    mate = {"col": c, "rep": 1 - r}
    others = [{"col": lax.rem(c + d, cols), "rep": r} for d in range(1, cols)]
    greet([mate] + others)
    order = [(k, d) for k in range(pieces) for d in range(1, cols)]
    order += [(k, 0) for k in range(pieces)]
    near, far, across, share, onward = {}, {}, {}, {}, {}
    for k, d in order:
        at = pl.ds(k * size, size)
        slot = lax.rem(c + d, cols) * reps + 1 - r
        near[k, d] = remote(
            p_ref.at[slot, at], a_ref.at[d, at], a_s.at[d, k], a_r.at[d, k], mate
        )
        near[k, d].start()
    for k, d in order:
        if d == 0:
            continue
        at = pl.ds(k * size, size)
        slot = lax.rem(c + d, cols) * reps + r
        near[k, d].wait_recv()
        s_ref[d - 1, at] = p_ref[slot, at] + a_ref[d, at]
        far[k, d] = remote(
            s_ref.at[d - 1, at], b_ref.at[d - 1, at], b_s.at[d - 1, k], b_r.at[d - 1, k], others[d - 1]
        )
        far[k, d].start()
    for k in range(pieces):
        at = pl.ds(k * size, size)
        near[k, 0].wait_recv()
        total = p_ref[me, at] + a_ref[0, at]
        for d in range(1, cols):
            far[k, d].wait_recv()
            total = total + b_ref[d - 1, at]
        out_ref[me, at] = total
        for d in range(1, cols):
            across[k, d] = remote(
                out_ref.at[me, at], out_ref.at[me, at], xs.at[d - 1, k], xr.at[d - 1, k], others[d - 1]
            )
            across[k, d].start()
        share[k] = remote(out_ref.at[me, at], out_ref.at[me, at], ps.at[k], pr.at[k], mate)
        share[k].start()
    for (k, d), copy in across.items():
        at = pl.ds(k * size, size)
        copy.wait_recv()
        slot = lax.rem(c + cols - d, cols) * reps + r
        onward[k, d] = remote(
            out_ref.at[slot, at], out_ref.at[slot, at], fs.at[d - 1, k], fr.at[d - 1, k], mate
        )
        onward[k, d].start()
    for copies in (near, far, across):
        for copy in copies.values():
            copy.wait_send()
    for copies in (share, onward):
        for copy in copies.values():
            copy.wait()


def total(parts, collective_id):
    cols, reps = lax.axis_size("col"), lax.axis_size("rep")
    if reps != 2 or cols < 2:
        return lax.psum(parts, ("col", "rep"))
    shape, kind = parts.shape[1:], parts.dtype
    pieces, _ = chunks_of(shape[0])
    dma = pltpu.SemaphoreType.DMA
    return pl.pallas_call(
        total_kernel,
        out_shape=jax.ShapeDtypeStruct(parts.shape, kind),
        in_specs=[pl.BlockSpec(memory_space=pltpu.VMEM)],
        out_specs=pl.BlockSpec(memory_space=pltpu.VMEM),
        scratch_shapes=[
            pltpu.VMEM((cols,) + shape, kind),
            pltpu.VMEM((cols - 1,) + shape, kind),
            pltpu.VMEM((cols - 1,) + shape, kind),
            dma((cols, pieces)),
            dma((cols, pieces)),
        ]
        + [dma((cols - 1, pieces))] * 6
        + [dma((pieces,))] * 2,
        compiler_params=pltpu.CompilerParams(
            collective_id=collective_id, has_side_effects=True, vmem_limit_bytes=VMEM_LIMIT
        ),
        name="total",
    )(parts)


def move_kernel(o_ref, code_ref, out_ref, arrived_ref, zs, zr, cs, cr, xs, xr, fs, fr, ps, pr, local):
    cols, reps, c, r = position()
    ntok, t = lax.axis_size("tok"), lax.axis_index("tok")
    me = c * reps + r
    mate = {"col": c, "rep": 1 - r}
    others = [{"col": lax.rem(c + d, cols), "rep": r} for d in range(1, cols)]
    peers = [{"tok": lax.rem(t + e, ntok)} for e in range(1, ntok)]
    greet([mate] + others + peers)
    along, codes, across, share, onward = [], [], {}, [], []
    for e in range(1, ntok):
        target = lax.rem(t + e, ntok)
        copy = remote(o_ref.at[target], out_ref.at[t, me], zs.at[e - 1], zr.at[e - 1], peers[e - 1])
        copy.start()
        along.append(copy)
        copy = remote(
            code_ref.at[target], arrived_ref.at[t], cs.at[e - 1], cr.at[e - 1], peers[e - 1]
        )
        copy.start()
        codes.append(copy)
    keep = pltpu.make_async_copy(o_ref.at[t], out_ref.at[t, me], local.at[0])
    keep.start()
    keep_code = pltpu.make_async_copy(code_ref.at[t], arrived_ref.at[t], local.at[1])
    keep_code.start()

    def hand_on(e):
        u = lax.rem(t + ntok - e, ntok)
        for d in range(1, cols):
            across[e, d].wait_recv()
            slot = lax.rem(c + cols - d, cols) * reps + r
            copy = remote(
                out_ref.at[u, slot], out_ref.at[u, slot], fs.at[e, d - 1], fr.at[e, d - 1], mate
            )
            copy.start()
            onward.append(copy)

    for e in range(ntok):
        u = lax.rem(t + ntok - e, ntok)
        if e:
            along[e - 1].wait_recv()
        origin = out_ref.at[u, me] if e else o_ref.at[t]
        for d in range(1, cols):
            across[e, d] = remote(
                origin, out_ref.at[u, me], xs.at[e, d - 1], xr.at[e, d - 1], others[d - 1]
            )
            across[e, d].start()
        copy = remote(origin, out_ref.at[u, me], ps.at[e], pr.at[e], mate)
        copy.start()
        share.append(copy)
        if e:
            hand_on(e - 1)
    hand_on(ntok - 1)
    keep.wait()
    keep_code.wait()
    for copy in along + list(across.values()):
        copy.wait_send()
    for copy in codes + share + onward:
        copy.wait()


def move(outgoing, codes, collective_id):
    cols, reps, ntok = lax.axis_size("col"), lax.axis_size("rep"), lax.axis_size("tok")
    if reps != 2 or cols < 2 or ntok < 2:
        incoming = lax.all_to_all(outgoing, "tok", split_axis=0, concat_axis=0, tiled=True)
        arrived = lax.all_to_all(codes, "tok", split_axis=0, concat_axis=0, tiled=True)
        return lax.all_gather(incoming, ("col", "rep"), axis=1), arrived
    dma = pltpu.SemaphoreType.DMA
    shape = (ntok, cols * reps) + outgoing.shape[1:]
    return pl.pallas_call(
        move_kernel,
        out_shape=(
            jax.ShapeDtypeStruct(shape, outgoing.dtype),
            jax.ShapeDtypeStruct(codes.shape, codes.dtype),
        ),
        in_specs=[pl.BlockSpec(memory_space=pltpu.VMEM)] * 2,
        out_specs=[pl.BlockSpec(memory_space=pltpu.VMEM)] * 2,
        scratch_shapes=[dma((ntok - 1,))] * 4
        + [dma((ntok, cols - 1))] * 4
        + [dma((ntok,))] * 2
        + [dma((2,))],
        compiler_params=pltpu.CompilerParams(
            collective_id=collective_id, has_side_effects=True, vmem_limit_bytes=VMEM_LIMIT
        ),
        name="move",
    )(outgoing, codes)


def pick_kernel(index_ref, x_ref, out_ref):
    for j in range(out_ref.shape[0]):
        out_ref[j] = x_ref[index_ref[j]]


def pick(blocks, index):
    return pl.pallas_call(
        pick_kernel,
        out_shape=jax.ShapeDtypeStruct(index.shape + blocks.shape[1:], blocks.dtype),
        in_specs=[pl.BlockSpec(memory_space=pltpu.SMEM), pl.BlockSpec(memory_space=pltpu.VMEM)],
        out_specs=pl.BlockSpec(memory_space=pltpu.VMEM),
        name="pick",
    )(index, blocks)


def attention_layer(blocks, source, layer, w_qkv, w_out, attn_gain, collective_id):
    group = blocks.shape[1]
    terms = attend(blocks, source, attn_gain[layer], w_qkv[layer], w_out[layer], group)
    rows, width = terms.shape
    return total(terms.reshape(group, rows // group, width), collective_id).reshape(rows, width)


def mlp_kernel(x_ref, gain_ref, up_ref, down_ref, share, out_ref):
    x = x_ref[...]
    hidden = dot3(split(layer_norm(x, gain_ref[...])), split(up_ref[...]))
    hidden = 0.5 * hidden * (1.0 + lax.erf(hidden * (0.5**0.5)))
    total = dot3(split(hidden), split(down_ref[...])) + x * share
    width = out_ref.shape[-1]
    for j in range(out_ref.shape[0]):
        out_ref[j] = total[:, j * width : (j + 1) * width]


def mlp_partial(stream, layer, w_up, w_down, mlp_gain, slots):
    rows, width = stream.shape
    tile = min(256, rows)
    hidden = w_up.shape[-1]
    group = lax.axis_size("col") * lax.axis_size("rep")

    def kernel(x_ref, gain_ref, up_ref, down_ref, out_ref):
        mlp_kernel(x_ref, gain_ref, up_ref, down_ref, 1.0 / group, out_ref)

    return pl.pallas_call(
        kernel,
        grid=(rows // tile,),
        in_specs=[
            pl.BlockSpec((tile, width), lambda i: (i, 0)),
            pl.BlockSpec((1, width), lambda i: (0, 0)),
            pl.BlockSpec((width, hidden), lambda i: (0, 0)),
            pl.BlockSpec((hidden, width), lambda i: (0, 0)),
        ],
        out_specs=pl.BlockSpec((slots, tile, width // slots), lambda i: (0, i, 0)),
        out_shape=jax.ShapeDtypeStruct((slots, rows, width // slots), jnp.float32),
        compiler_params=pltpu.CompilerParams(vmem_limit_bytes=48 * 1024 * 1024),
        name="mlp",
    )(stream, mlp_gain[layer][None, :], w_up[layer], w_down[layer])


def routes(dest_device, dest_slot):
    count = dest_device.shape[0]
    peers = lax.axis_size("tok")
    capacity = max(2, (count + peers - 4) // (peers - 1))
    order = jnp.arange(count, dtype=jnp.int32)
    earlier = (dest_device[:, None] == dest_device[None, :]) & (order[None, :] < order[:, None])
    place = dest_device * capacity + jnp.sum(earlier.astype(jnp.int32), axis=1)
    chosen = jnp.arange(peers * capacity, dtype=jnp.int32)[:, None] == place[None, :]
    index = jnp.sum(jnp.where(chosen, order[None, :], 0), axis=1)
    code = jnp.sum(jnp.where(chosen, dest_slot[None, :] + 1, 0), axis=1)
    code = jnp.pad(code.reshape(peers, capacity), ((0, 0), (0, 128 - capacity)))
    code = jnp.broadcast_to(code[:, None, :], (peers, 8, 128)).astype(jnp.float32)
    return index, code, capacity


def raster_cells(extended, depth_weight, point_weight, gain_row):
    row_count = extended.shape[0] - 2
    col_count = extended.shape[1] - 2
    channels = extended.shape[2]
    normed = (
        extended
        * lax.rsqrt(jnp.mean(extended * extended, axis=-1, keepdims=True) + EPSILON)
        * gain_row
    )
    mixed = jnp.zeros((row_count, col_count, channels), jnp.float32)
    for a in range(3):
        for b in range(3):
            mixed = mixed + normed[a : a + row_count, b : b + col_count] * depth_weight[a, b]
    combined = matmul(mixed.reshape(row_count * col_count, channels), point_weight)
    combined = combined.reshape(row_count, col_count, 2 * channels)
    centre = extended[1:-1, 1:-1]
    return centre + combined[..., :channels] * jax.nn.sigmoid(combined[..., channels:])


HALO = 2


def extended_cells(tok, members, rep_rows, full_width):
    cols, reps = members
    tile = []
    for col in range(cols):
        for rep in range(reps):
            y = rep * rep_rows - HALO + jnp.arange(rep_rows + 2 * HALO, dtype=jnp.int32)[:, None]
            x = col * TC - HALO + jnp.arange(TC + 2 * HALO, dtype=jnp.int32)[None, :]
            good = (y >= 0) & (y < TR) & (x >= 0) & (x < full_width)
            tile.append(jnp.where(good, (tok * TR + y) * full_width + x, -2).reshape(-1))
    return jnp.concatenate(tile)


def pool(partial, pillar, cells):
    onehot = (cells[:, None] == pillar[None, :]).astype(jnp.float32)
    return matmul(onehot, partial)


def exchange_rows(tile, ntok, reps):
    count = ntok * reps
    rep = lax.axis_index("rep")
    forward = [(i, i + 1) for i in range(count - 1)]
    backward = [(i + 1, i) for i in range(count - 1)]
    above = lax.ppermute(tile[-2 * HALO : -HALO], ("tok", "rep"), forward)
    below = lax.ppermute(tile[HALO : 2 * HALO], ("tok", "rep"), backward)
    above = jnp.where(rep == 0, above, tile[:HALO])
    below = jnp.where(rep == reps - 1, below, tile[-HALO:])
    return jnp.concatenate([above, tile[HALO:-HALO], below], axis=0)


def on_device(
    tokens,
    w_qkv,
    w_out,
    w_up,
    w_down,
    attn_gain,
    mlp_gain,
    dest_device,
    dest_slot,
    pillar,
    depth_weight,
    point_weight,
    raster_gain,
):
    members = (lax.axis_size("col"), lax.axis_size("rep"))
    group = members[0] * members[1]
    ntok = lax.axis_size("tok")
    block_count = dest_device.shape[0]
    order = jnp.arange(block_count, dtype=jnp.int32)
    index, codes, capacity = routes(dest_device, dest_slot)
    width = tokens.shape[1]
    blocks = gather(tokens, 1).reshape(1, group, block_count, -1, width)
    stream = attention_layer(blocks, order, 0, w_qkv, w_out, attn_gain, 2)
    share = scatter(mlp_partial(stream, 0, w_up, w_down, mlp_gain, group), 3)
    outgoing = pick(share.reshape(block_count, -1, width), index)
    outgoing = outgoing.reshape(ntok, -1, width)
    moved, arrived = move(outgoing, codes, 4)
    blocks = moved.reshape(ntok, group, capacity, -1, width)
    held = arrived[:, 0, :capacity].reshape(-1).astype(jnp.int32)
    found = held[None, :] == order[:, None] + 1
    source = jnp.sum(jnp.where(found, jnp.arange(held.shape[0], dtype=jnp.int32)[None, :], 0), axis=1)
    stream = attention_layer(blocks, source, 1, w_qkv, w_out, attn_gain, 5)
    partial = mlp_partial(stream, 1, w_up, w_down, mlp_gain, 1)[0]

    rep_rows = TR // members[1]
    full_width = TC * members[0]
    cells = extended_cells(lax.axis_index("tok"), members, rep_rows, full_width)
    pooled = pool(partial, pillar, cells)
    parts = pooled.reshape(group, -1, pooled.shape[1])
    edge = HALO * (TC + 2 * HALO)
    inside_kernel = members[0] > 1 and members[1] == 2 and ntok > 1 and edge % 8 == 0
    tile = scatter(parts, 6, edge if inside_kernel else 0)
    tile = tile.reshape(rep_rows + 2 * HALO, TC + 2 * HALO, -1)
    if not inside_kernel:
        tile = exchange_rows(tile, ntok, members[1])
    first = raster_cells(tile, depth_weight[0], point_weight[0], raster_gain[0])
    y = lax.axis_index(("tok", "rep")) * rep_rows - 1 + jnp.arange(rep_rows + 2)[:, None, None]
    x = lax.axis_index("col") * TC - 1 + jnp.arange(TC + 2)[None, :, None]
    inside = (y >= 0) & (y < TR * ntok) & (x >= 0) & (x < full_width)
    first = jnp.where(inside, first, 0.0)
    return raster_cells(first, depth_weight[1], point_weight[1], raster_gain[1])


def solution(mesh):
    placed = (
        P(("scene", "tok"), ("col", "rep")),
        P(None, None, None, ("col", "rep")),
        P(None, ("col", "rep"), None),
        P(None, None, ("col", "rep")),
        P(None, ("col", "rep"), None),
        P(),
        P(),
        P(("scene", "tok")),
        P(("scene", "tok")),
        P(("scene", "tok")),
        P(),
        P(),
        P(),
    )
    return jax.shard_map(
        on_device,
        mesh=mesh,
        in_specs=placed,
        out_specs=P(("scene", "tok", "rep"), "col", None),
        check_vma=False,
    )
```

profile of v0, /device:TPU:0, one launch (start us, length us, event | category | flops | bytes accessed | tf_op | source)
XLA Modules:
  0.0 250.7 jit_solution(11102338712293790555)
XLA Ops:
  0.0 1.0 convert_reduce_fusion
  2.3 19.2 %gather.1 = f32[4,1024,128]{2,1,0:T(8,128)} custom-call(f32[1024,128]{1,0:T(8,128)} %x_ref.1), custom_call_target="tpu_custom_call" | custom-call | tf_op jit(solution)/shard_map/gather/pallas_call | solution.py:217
  21.6 0.9 copy-done.9
  23.2 27.2 %attend.2 = f32[1024,512]{1,0:T(8,128)S(1)} custom-call(s32[16]{0:T(128)S(1)} %iota.86.source_ref, f32[1,4,16,64,128]{4,3,2,1,0:T(8,128)S(1)} %bitcast.60, f32[1,512]{1,0:T(1,128)S(1)} %get-tuple-element.46.gain_ref, f32[3,512,128]{2,1,0:T(8,128)S(1)} %get-tuple-element.18.w_ref, f32[128,512]{1,0:T(8,128)S(1)} %get-tuple-element.20.o_ref), custom_call_target="tpu_custom_call" | custom-call | tf_op jit(solution)/shard_map/attend/pallas_call | solution.py:114
  50.4 1.3 copy-done.1
  51.8 31.4 %total.2 = f32[4,256,512]{2,1,0:T(8,128)} custom-call(f32[4,256,512]{2,1,0:T(8,128)} %bitcast.61), custom_call_target="tpu_custom_call" | custom-call | tf_op jit(solution)/shard_map/total/pallas_call | solution.py:385
  83.7 6.6 %mlp.2.p_ref = f32[4,1024,128]{2,1,0:T(8,128)S(1)} custom-call(f32[1024,512]{1,0:T(8,128)} %bitcast.64, f32[1,512]{1,0:T(1,128)S(1)} %get-tuple-element.44.gain_ref, f32[512,512]{1,0:T(8,128)S(1)} %get-tuple-element.57.up_ref, f32[512,512]{1,0:T(8,128)S(1)} %get-tuple-element.14.down_ref), custom_call_target="tpu_custom_call" | custom-call | tf_op jit(solution)/shard_map/mlp/pallas_call | solution.py:533
  90.3 1.3 copy-done.2
  91.7 18.2 %scatter.2 = f32[1024,128]{1,0:T(8,128)} custom-call(f32[4,1024,128]{2,1,0:T(8,128)} %copy-done.2), custom_call_target="tpu_custom_call" | custom-call | tf_op jit(solution)/shard_map/scatter/pallas_call | solution.py:294
  109.9 1.9 pick.1
  112.6 27.9 %move.1 = (f32[4,4,320,128]{3,2,1,0:T(8,128)}, f32[4,8,128]{2,1,0:T(8,128)}) custom-call(f32[4,320,128]{2,1,0:T(8,128)} %bitcast.66, f32[4,8,128]{2,1,0:T(8,128)} %broadcast_in_dim.85.code_ref), custom_call_target="tpu_custom_call" | custom-call | tf_op jit(solution)/shard_map/move/pallas_call | solution.py:473
  141.5 1.7 copy-done.4
  143.2 27.2 %attend.3 = f32[1024,512]{1,0:T(8,128)S(1)} custom-call(s32[16]{0:T(128)S(1)} %select_reduce_fusion.source_ref, f32[4,4,5,64,128]{4,3,2,1,0:T(8,128)S(1)} %bitcast.63, f32[1,512]{1,0:T(1,128)S(1)} %get-tuple-element.45.gain_ref, f32[3,512,128]{2,1,0:T(8,128)S(1)} %get-tuple-element.17.w_ref, f32[128,512]{1,0:T(8,128)S(1)} %get-tuple-element.19.o_ref), custom_call_target="tpu_custom_call" | custom-call | tf_op jit(solution)/shard_map/attend/pallas_call | solution.py:114
  170.4 1.3 copy-done.3
  171.7 31.3 %total.3 = f32[4,256,512]{2,1,0:T(8,128)} custom-call(f32[4,256,512]{2,1,0:T(8,128)} %bitcast.62), custom_call_target="tpu_custom_call" | custom-call | tf_op jit(solution)/shard_map/total/pallas_call | solution.py:385
  203.0 6.8 %mlp.3 = f32[1,1024,512]{2,1,0:T(8,128)S(1)} custom-call(f32[1024,512]{1,0:T(8,128)} %bitcast.65, f32[1,512]{1,0:T(1,128)S(1)} %get-tuple-element.43.gain_ref, f32[512,512]{1,0:T(8,128)S(1)} %get-tuple-element.58.up_ref, f32[512,512]{1,0:T(8,128)S(1)} %get-tuple-element.13.down_ref), custom_call_target="tpu_custom_call" | custom-call | tf_op jit(solution)/shard_map/mlp/pallas_call | solution.py:533
  209.8 1.3 copy-done.5
  211.8 5.1 %fusion.p_ref = f32[4,240,512]{2,1,0:T(8,128)} fusion(f32[1,1024,512]{2,1,0:T(8,128)} %copy-done.5, s32[1024]{0:T(1024)S(1)} %copy-done.14, s32[4,240]{1,0:T(4,128)S(1)} %eq.59), kind=kOutput, calls=%fused_computation | convolution fusion | flops 3020881920 | bytes 4071168 | tf_op jit(solution)/shard_map/dot_general | solution.py:140
  216.9 24.4 %scatter.3 = f32[240,512]{1,0:T(8,128)} custom-call(f32[4,240,512]{2,1,0:T(8,128)} %fusion.p_ref), custom_call_target="tpu_custom_call" | custom-call | tf_op jit(solution)/shard_map/scatter/pallas_call | solution.py:294
  241.3 1.1 reshape.275
  242.4 1.1 multiply_reduce_fusion.1
  243.9 3.0 %fusion.4 = f32[10,18,1024]{2,1,0:T(8,128)S(1)} fusion(f32[2,512,1024]{2,1,0:T(8,128)} %param.24, f32[12,20,512]{2,1,0:T(8,128)S(1)} %multiply_multiply_fusion, f32[512]{0:T(512)S(1)} %bitcast.71, f32[512]{0:T(512)S(1)} %bitcast.72, f32[512]{0:T(512)S(1)} %bitcast.73, f32[512]{0:T(512)S(1)} %bitcast.74, f32[512]{0:T(512)S(1)} %bitcast.75, ...), kind=kOutput, calls=%fused_computation.4 | convolution fusion | flops 567797760 | bytes 7276544 | tf_op jit(solution)/shard_map/dot_general | solution.py:140
  247.4 2.5 fusion.2
  249.9 0.8 fusion.37
  (65 shorter events, 5.8 us)
Async XLA Ops:
  0.0 21.4 %copy-start.11 = (f32[2,512]{1,0:T(2,128)S(1)}, f32[2,512]{1,0:T(2,128)}, u32[]{:S(2)}) copy-start(f32[2,512]{1,0:T(2,128)} %param.18) | copy-start | bytes 12292
  0.0 21.5 %copy-start.8 = (f32[2,3,512,128]{3,2,1,0:T(8,128)S(1)}, f32[2,3,512,128]{3,2,1,0:T(8,128)}, u32[]{:S(2)}) copy-start(f32[2,3,512,128]{3,2,1,0:T(8,128)} %param.14) | copy-start | bytes 4718596
  21.4 1.0 copy-start.9
  21.5 1.7 copy-start
  23.2 60.0 %copy-start.12 = (f32[2,512]{1,0:T(2,128)S(1)}, f32[2,512]{1,0:T(2,128)}, u32[]{:S(2)}) copy-start(f32[2,512]{1,0:T(2,128)} %param.19) | copy-start | bytes 12292
  50.4 1.3 copy-start.1
  51.8 31.5 %copy-start.6 = (f32[2,512,512]{2,1,0:T(8,128)S(1)}, f32[2,512,512]{2,1,0:T(8,128)}, u32[]{:S(2)}) copy-start(f32[2,512,512]{2,1,0:T(8,128)} %param.17) | copy-start | bytes 6291460
  51.8 31.5 %copy-start.7 = (f32[2,512,512]{2,1,0:T(8,128)S(1)}, f32[2,512,512]{2,1,0:T(8,128)}, u32[]{:S(2)}) copy-start(f32[2,512,512]{2,1,0:T(8,128)} %param.16) | copy-start | bytes 6291460
  90.3 1.3 copy-start.2
  141.4 1.7 copy-start.4
  170.4 1.3 copy-start.3
  203.0 8.7 %copy-start.14 = (s32[1024]{0:T(1024)S(1)}, s32[1024]{0:T(1024)}, u32[]{:S(2)}) copy-start(s32[1024]{0:T(1024)} %param.22) | copy-start | bytes 12292
  209.8 1.3 copy-start.5
  216.9 25.5 %copy-start.13 = (f32[2,512]{1,0:T(2,128)S(1)}, f32[2,512]{1,0:T(2,128)}, u32[]{:S(2)}) copy-start(f32[2,512]{1,0:T(2,128)} %param.25) | copy-start | bytes 12292
  216.9 26.9 %copy-start.10 = (f32[2,3,3,512]{3,0,2,1:T(2,128)S(1)}, f32[2,3,3,512]{3,0,2,1:T(2,128)}, u32[]{:S(2)}) copy-start(f32[2,3,3,512]{3,0,2,1:T(2,128)} %param.23) | copy-start | bytes 110596
where the time goes:
time: 251 us
  Pallas kernels  222 us (88%)
  local copies, waits for them, and re-layouts  11.7 us (5%)
  matrix products  10.6 us (4%)
  other arithmetic  5.95 us (2%)
    pallas_call x2, Pallas kernels, total(): pl.pallas_call(total_kernel, out_shape=jax.ShapeDtypeStruct(parts.shape,...  62.7 us
    pallas_call x2, Pallas kernels, attend(): pl.pallas_call(functools.partial(attention_kernel, 1.0 / group), grid_spe...  54.4 us
    pallas_call x2, Pallas kernels, scatter(): pl.pallas_call(functools.partial(scatter_kernel, edge), out_shape=jax.Sha...  42.6 us
    pallas_call x1, Pallas kernels, move(): pl.pallas_call(move_kernel, out_shape=(jax.ShapeDtypeStruct(shape, outgoi...  27.9 us
    pallas_call x1, Pallas kernels, gather(): pl.pallas_call(gather_kernel, out_shape=jax.ShapeDtypeStruct((cols * reps...  19.2 us
    pallas_call x2, Pallas kernels, mlp_partial(): pl.pallas_call(kernel, grid=(rows // tile,), in_specs=[pl.BlockSpec((tile...  13.4 us
    dot_general x3, matrix products, matmul(): jnp.dot(left, right, precision=MATMUL_PRECISION, preferred_element_type=j...  10.6 us
    unnamed x31, local copies, waits for them, and re-layouts  8.68 us

commit v1 on v0

--- a/solution.py
+++ b/solution.py
@@ -546,6 +546,310 @@
     )(stream, mlp_gain[layer][None, :], w_up[layer], w_down[layer])
 
 
+def gelu(values):
+    return 0.5 * values * (1.0 + lax.erf(values * (0.5**0.5)))
+
+
+NEAR, FAR, SHARE, NEAR2, FAR2, ACROSS, OVER, RELAY = range(8)
+
+
+def layer_kernel(layer, first, heads, chunk, *refs):
+    refs = list(refs)
+    source_ref = None if first else refs.pop(0)
+    x_ref, ga_ref, gm_ref, wqkv_hbm, wo_hbm, wu_hbm, wd_hbm, out_ref = refs[:8]
+    (
+        wqkv_f, wo_f, wu_f, wd_f, wqkv_s, wo_s, wu_s, wd_s,
+        q_s, k_s, v_s, att_s, p_s, n1_s, s1_s, f1_s, a_s, sem, wsem,
+    ) = refs[8:27]
+    rest = refs[27:]
+    cols, reps, c, r = position()
+    me = c * reps + r
+    mate, peer = {"rep": 1 - r}, {"col": 1 - c}
+    lanes = q_s.shape[-1] // 2
+    width = a_s.shape[-1]
+    rows = a_s.shape[0]
+    n = rows // chunk
+    half_rows = chunk // 2
+    half_lanes = lanes // 2
+    half_heads = heads // 2
+
+    def piece(i, size):
+        return pl.ds(pl.multiple_of(i * size, size), size)
+
+    def sent(kind, i, src, dst, device):
+        return remote(src, dst, sem.at[kind, 0, i], sem.at[kind, 1, i], device)
+
+    loads = [
+        pltpu.make_async_copy(src.at[layer], dst, wsem.at[j])
+        for j, (src, dst) in enumerate(
+            ((wqkv_hbm, wqkv_f), (wo_hbm, wo_f), (wu_hbm, wu_f), (wd_hbm, wd_f))
+        )
+    ]
+    for load in loads:
+        load.start()
+    greet([mate, peer])
+
+    if first:
+        g_s, m_s, n2_s, s2_s, f2_s = rest
+
+        def across(i):
+            at = piece(i, chunk)
+            return sent(ACROSS, i, x_ref.at[at], g_s.at[me, at], peer)
+
+        def over(i):
+            at = piece(i, chunk)
+            return sent(OVER, i, x_ref.at[at], g_s.at[me, at], mate)
+
+        def relay(i):
+            at = piece(i, chunk)
+            slot = (1 - c) * reps + r
+            return sent(RELAY, i, g_s.at[slot, at], g_s.at[slot, at], mate)
+
+        for i in range(n):
+            across(i).start()
+        for i in range(n):
+            over(i).start()
+        g_s[me] = x_ref[...]
+
+        def stream_rows(start, count):
+            at = pl.ds(pl.multiple_of(start, count), count)
+            return jnp.concatenate([g_s[j, at] for j in range(cols * reps)], axis=-1)
+
+    else:
+        each, block = x_ref.shape[2:4]
+
+        def stream_rows(start, count):
+            parts = []
+            for m in range(count // block):
+                at = source_ref[start // block + m]
+                places = [x_ref[at // each, j, at % each] for j in range(cols * reps)]
+                parts.append(jnp.concatenate(places, axis=-1))
+            return jnp.concatenate(parts, axis=0)
+
+    for j, (load, src, dst) in enumerate(
+        zip(loads, (wqkv_f, wo_f, wu_f, wd_f), (wqkv_s, wo_s, wu_s, wd_s))
+    ):
+        load.wait()
+        if j == 0:
+            for m in range(3):
+                dst[0, m], dst[1, m] = split(src[m])
+        else:
+            dst[0], dst[1] = split(src[...])
+
+    lane = lax.broadcasted_iota(jnp.int32, (1, lanes), 1)
+
+    def project(i):
+        at = piece(i, chunk)
+        normed = split(layer_norm(stream_rows(i * chunk, chunk), ga_ref[...]))
+        q = dot3(normed, (wqkv_s[0, 0], wqkv_s[1, 0])) * (HD ** (-0.5) * math.log2(math.e))
+        k = dot3(normed, (wqkv_s[0, 1], wqkv_s[1, 1]))
+        v = dot3(normed, (wqkv_s[0, 2], wqkv_s[1, 2]))
+        qh, ql = split(q)
+        kh, kl = [part.astype(jnp.float32) for part in split(k)]
+        vh, vl = [part.astype(jnp.float32) for part in split(v)]
+        lower = lane < half_lanes
+        qf, qlf = qh.astype(jnp.float32), ql.astype(jnp.float32)
+        q_s[0, at, :lanes] = qh
+        q_s[1, at, :lanes] = qh
+        q_s[0, at, lanes:] = jnp.where(lower, qf, pltpu.roll(qlf, half_lanes, 1)).astype(jnp.bfloat16)
+        q_s[1, at, lanes:] = jnp.where(lower, pltpu.roll(qf, half_lanes, 1), qlf).astype(jnp.bfloat16)
+        kh_r, kl_r = pltpu.roll(kh, half_lanes, 1), pltpu.roll(kl, half_lanes, 1)
+        for h in range(heads):
+            own = lane // HD == h
+            other = lane // HD == (h + half_heads) % heads
+            k_s[h, at, :lanes] = jnp.where(own, kh, 0.0).astype(jnp.bfloat16)
+            if h < half_heads:
+                mixed = jnp.where(own, kl, jnp.where(other, kh_r, 0.0))
+            else:
+                mixed = jnp.where(own, kh, jnp.where(other, kl_r, 0.0))
+            k_s[h, at, lanes:] = mixed.astype(jnp.bfloat16)
+            v_s[h, at, :lanes] = jnp.where(own, vh, 0.0).astype(jnp.bfloat16)
+            v_s[h, at, lanes:] = jnp.where(own, vl, 1.0).astype(jnp.bfloat16)
+
+    def gather_step(i, carry):
+        if first:
+            @pl.when(i < n)
+            def _():
+                across(i).wait_recv()
+                relay(i).start()
+
+            @pl.when(i > 0)
+            def _():
+                over(i - 1).wait_recv()
+                relay(i - 1).wait_recv()
+                project(i - 1)
+
+        else:
+            project(i)
+        return carry
+
+    lax.fori_loop(0, n + 1 if first else n, gather_step, 0)
+
+    def near(i):
+        return sent(
+            NEAR, i, p_s.at[pl.ds(pl.multiple_of(i * chunk + (1 - r) * half_rows, half_rows), half_rows)],
+            n1_s.at[piece(i, half_rows)], mate,
+        )
+
+    def far(i):
+        at = piece(i, half_rows)
+        return sent(FAR, i, s1_s.at[at], f1_s.at[at], peer)
+
+    def own_half(i):
+        return pl.ds(pl.multiple_of(i * chunk + r * half_rows, half_rows), half_rows)
+
+    def share(i):
+        at = own_half(i)
+        return sent(SHARE, i, a_s.at[at], a_s.at[at], mate)
+
+    def attention(k):
+        i, half = k // 2, k % 2
+        at = piece(i, chunk)
+        total = jnp.zeros((chunk, lanes), jnp.float32)
+        for m in range(half_heads):
+            h = half * half_heads + m
+            scores = bdot(q_s[half, at, :], k_s[h], (((1,), (1,)), ((), ())))
+            weights = jnp.exp2(scores - jnp.max(scores, axis=-1, keepdims=True))
+            wh, wl = split(weights)
+            sums = bdot(wh, v_s[h]) + bdot(wl, v_s[h])
+            top, low = sums[:, :lanes], sums[:, lanes:]
+            total += jnp.where(lane // HD == h, (top + low) / pltpu.roll(low, half_lanes, 1), 0.0)
+        att_s[half] = total
+
+    def finish(i):
+        p_s[piece(i, chunk)] = dot3(split(att_s[0] + att_s[1]), (wo_s[0], wo_s[1]))
+        near(i).start()
+
+    def reduce_near(i):
+        near(i).wait_recv()
+        at = piece(i, half_rows)
+        s1_s[at] = p_s[own_half(i)] + n1_s[at]
+        far(i).start()
+
+    def reduce_far(i):
+        far(i).wait_recv()
+        at = piece(i, half_rows)
+        stream = stream_rows(i * chunk + r * half_rows, half_rows)
+        a_s[own_half(i)] = (s1_s[at] + f1_s[at]) + stream
+        share(i).start()
+
+    def feed(i):
+        share(i).wait_recv()
+        at = piece(i, chunk)
+        x = a_s[at]
+        hidden = gelu(dot3(split(layer_norm(x, gm_ref[...])), (wu_s[0], wu_s[1])))
+        total = dot3(split(hidden), (wd_s[0], wd_s[1]))
+        if first:
+            for j in range(cols * reps):
+                m_s[j % reps, j // reps, at] = total[:, j * lanes : (j + 1) * lanes]
+            near2(i).start()
+        else:
+            out_ref[at] = total + x * (1.0 / (cols * reps))
+
+    def near2(i):
+        at = piece(i, chunk)
+        return sent(NEAR2, i, m_s.at[1 - r, :, at], n2_s.at[:, at], mate)
+
+    def far2(i):
+        at = piece(i, chunk)
+        return sent(FAR2, i, s2_s.at[at], f2_s.at[at], peer)
+
+    def scatter_near(i):
+        near2(i).wait_recv()
+        at = piece(i, chunk)
+        s2_s[at] = m_s[r, 1 - c, at] + n2_s[1 - c, at]
+        far2(i).start()
+
+    def scatter_far(i):
+        far2(i).wait_recv()
+        at = piece(i, chunk)
+        own = a_s[at, pl.ds(pl.multiple_of(me * lanes, lanes), lanes)]
+        out_ref[at] = (m_s[r, c, at] + n2_s[c, at]) + f2_s[at] + own
+
+    stages = [(9, scatter_far), (7, scatter_near), (6, feed), (5, reduce_far), (2, reduce_near), (1, finish)]
+    if not first:
+        stages = stages[2:]
+
+    def tick(k, carry):
+        @pl.when(k < 2 * n)
+        def _():
+            attention(k)
+
+        for offset, stage in stages:
+            @pl.when((k >= offset) & (k < offset + 2 * n) & ((k - offset) % 2 == 0))
+            def _(offset=offset, stage=stage):
+                stage((k - offset) // 2)
+
+        return carry
+
+    lax.fori_loop(0, 2 * n + stages[0][0] - 1, tick, 0)
+
+    kinds = [near, far, share] + ([near2, far2, across, over, relay] if first else [])
+    for copy in kinds:
+        for i in range(n):
+            copy(i).wait_send()
+
+
+def run_layer(layer, first, x, source, w_qkv, w_out, w_up, w_down, attn_gain, mlp_gain, collective_id):
+    cols, reps = lax.axis_size("col"), lax.axis_size("rep")
+    group = cols * reps
+    lanes = w_qkv.shape[-1]
+    width = w_qkv.shape[-2]
+    hidden = w_up.shape[-1]
+    heads = lanes // HD
+    rows = PATCH
+    chunk = min(256, rows)
+    n = rows // chunk
+    dma, f32, b16 = pltpu.SemaphoreType.DMA, jnp.float32, jnp.bfloat16
+    vmem = pl.BlockSpec(memory_space=pltpu.VMEM)
+    hbm = pl.BlockSpec(memory_space=pl.ANY)
+    scratch = [
+        pltpu.VMEM((3, width, lanes), f32),
+        pltpu.VMEM((lanes, width), f32),
+        pltpu.VMEM((width, hidden), f32),
+        pltpu.VMEM((hidden, width), f32),
+        pltpu.VMEM((2, 3, width, lanes), b16),
+        pltpu.VMEM((2, lanes, width), b16),
+        pltpu.VMEM((2, width, hidden), b16),
+        pltpu.VMEM((2, hidden, width), b16),
+        pltpu.VMEM((2, rows, 2 * lanes), b16),
+        pltpu.VMEM((heads, rows, 2 * lanes), b16),
+        pltpu.VMEM((heads, rows, 2 * lanes), b16),
+        pltpu.VMEM((2, chunk, lanes), f32),
+        pltpu.VMEM((rows, width), f32),
+        pltpu.VMEM((rows // 2, width), f32),
+        pltpu.VMEM((rows // 2, width), f32),
+        pltpu.VMEM((rows // 2, width), f32),
+        pltpu.VMEM((rows, width), f32),
+        dma((8 if first else 3, 2, n)),
+        dma((4,)),
+    ]
+    if first:
+        scratch += [
+            pltpu.VMEM((group, rows, lanes), f32),
+            pltpu.VMEM((reps, cols, rows, lanes), f32),
+            pltpu.VMEM((cols, rows, lanes), f32),
+            pltpu.VMEM((rows, lanes), f32),
+            pltpu.VMEM((rows, lanes), f32),
+        ]
+    operands = [x, attn_gain[layer][None, :], mlp_gain[layer][None, :], w_qkv, w_out, w_up, w_down]
+    specs = [vmem] * 3 + [hbm] * 4
+    if not first:
+        operands = [source] + operands
+        specs = [pl.BlockSpec(memory_space=pltpu.SMEM)] + specs
+    return pl.pallas_call(
+        functools.partial(layer_kernel, layer, first, heads, chunk),
+        out_shape=jax.ShapeDtypeStruct((rows, lanes if first else width), f32),
+        in_specs=specs,
+        out_specs=vmem,
+        scratch_shapes=scratch,
+        compiler_params=pltpu.CompilerParams(
+            collective_id=collective_id, has_side_effects=True, vmem_limit_bytes=VMEM_LIMIT
+        ),
+        name="first_layer" if first else "second_layer",
+    )(*operands)
+
+
 def routes(dest_device, dest_slot):
     count = dest_device.shape[0]
     peers = lax.axis_size("tok")
@@ -634,9 +938,15 @@
     order = jnp.arange(block_count, dtype=jnp.int32)
     index, codes, capacity = routes(dest_device, dest_slot)
     width = tokens.shape[1]
-    blocks = gather(tokens, 1).reshape(1, group, block_count, -1, width)
-    stream = attention_layer(blocks, order, 0, w_qkv, w_out, attn_gain, 2)
-    share = scatter(mlp_partial(stream, 0, w_up, w_down, mlp_gain, group), 3)
+    rows = tokens.shape[0]
+    pair = members == (2, 2) and rows == PATCH
+    weights = (w_qkv, w_out, w_up, w_down, attn_gain, mlp_gain)
+    if pair:
+        share = run_layer(0, True, tokens, None, *weights, 1)
+    else:
+        blocks = gather(tokens, 1).reshape(1, group, block_count, -1, width)
+        stream = attention_layer(blocks, order, 0, w_qkv, w_out, attn_gain, 2)
+        share = scatter(mlp_partial(stream, 0, w_up, w_down, mlp_gain, group), 3)
     outgoing = pick(share.reshape(block_count, -1, width), index)
     outgoing = outgoing.reshape(ntok, -1, width)
     moved, arrived = move(outgoing, codes, 4)
@@ -644,8 +954,11 @@
     held = arrived[:, 0, :capacity].reshape(-1).astype(jnp.int32)
     found = held[None, :] == order[:, None] + 1
     source = jnp.sum(jnp.where(found, jnp.arange(held.shape[0], dtype=jnp.int32)[None, :], 0), axis=1)
-    stream = attention_layer(blocks, source, 1, w_qkv, w_out, attn_gain, 5)
-    partial = mlp_partial(stream, 1, w_up, w_down, mlp_gain, 1)[0]
+    if pair:
+        partial = run_layer(1, False, blocks, source, *weights, 5)
+    else:
+        stream = attention_layer(blocks, source, 1, w_qkv, w_out, attn_gain, 5)
+        partial = mlp_partial(stream, 1, w_up, w_down, mlp_gain, 1)[0]
 
     rep_rows = TR // members[1]
     full_width = TC * members[0]

time: 251 us -> 188 us (0.75)
  Pallas kernels: 222 us -> 167 us
  local copies, waits for them, and re-layouts: 11.7 us -> 3.74 us
    pallas_call x7 -> x2, Pallas kernels: 150 us -> 115 us  [run_layer(): pl.pallas_call(functools.partial(layer_kernel, layer, first, heads, chunk...]
    pallas_call x2 -> x1, Pallas kernels: 42.6 us -> 23.3 us  [scatter(): pl.pallas_call(functools.partial(scatter_kernel, edge), out_shape=jax.Sha...]
    unnamed x31 -> x7, local copies, waits for them, and re-layouts: 8.68 us -> 0.03 us
where the time goes in v1:
time: 188 us
  Pallas kernels  167 us (89%)
  matrix products  10.6 us (6%)
  other arithmetic  6.41 us (3%)
  local copies, waits for them, and re-layouts  3.74 us (2%)
    pallas_call x2, Pallas kernels, run_layer(): pl.pallas_call(functools.partial(layer_kernel, layer, first, heads, chunk...  115 us
    pallas_call x1, Pallas kernels, move(): pl.pallas_call(move_kernel, out_shape=(jax.ShapeDtypeStruct(shape, outgoi...  26.6 us
    pallas_call x1, Pallas kernels, scatter(): pl.pallas_call(functools.partial(scatter_kernel, edge), out_shape=jax.Sha...  23.3 us
    dot_general x3, matrix products, matmul(): jnp.dot(left, right, precision=MATMUL_PRECISION, preferred_element_type=j...  10.6 us

profile of v1, /device:TPU:0, one launch (start us, length us, event | category | flops | bytes accessed | tf_op | source)
XLA Modules:
  0.0 187.6 jit_solution(1029094787207936466)
XLA Ops:
  0.0 0.9 convert_reduce_fusion
  0.9 0.7 multiply_add_fusion
  1.6 0.6 select_reduce_fusion.1
  2.2 1.4 fusion.79
  3.6 68.4 %first_layer.1 = f32[1024,128]{1,0:T(8,128)} custom-call(f32[1024,128]{1,0:T(8,128)} %refs_0_.1, f32[1,512]{1,0:T(1,128)} %get-tuple-element.49.refs_1_, f32[1,512]{1,0:T(1,128)} %get-tuple-element.36.refs_2_, f32[2,3,512,128]{3,2,1,0:T(8,128)} %refs_4_.3, f32[2,128,512]{2,1,0:T(8,128)} %refs_5_.3, f32[2,512,512]{2,1,0:T(8,128)} %refs_6_.3, ...), custom_call_target="tpu_custom_call" | custom-call | tf_op jit(solution)/shard_map/first_layer/pallas_call | solution.py:840
  72.0 1.9 %pick.1 = f32[20,64,128]{2,1,0:T(8,128)} custom-call(s32[20]{0:T(128)} %get-tuple-element.10.index_ref, f32[16,64,128]{2,1,0:T(8,128)} %bitcast.39), custom_call_target="tpu_custom_call" | custom-call | tf_op jit(solution)/shard_map/pick/pallas_call | solution.py:498
  73.9 0.1 reshape.241
  74.0 0.6 broadcast_in_dim.85.code_ref
  74.6 26.6 %move.1 = (f32[4,4,320,128]{3,2,1,0:T(8,128)}, f32[4,8,128]{2,1,0:T(8,128)}) custom-call(f32[4,320,128]{2,1,0:T(8,128)} %bitcast.38, f32[4,8,128]{2,1,0:T(8,128)} %broadcast_in_dim.85.code_ref), custom_call_target="tpu_custom_call" | custom-call | tf_op jit(solution)/shard_map/move/pallas_call | solution.py:473
  101.2 0.7 convert_reduce_fusion.1
  101.9 0.1 convert_element_type.20
  102.0 0.7 select_reduce_fusion.refs_0_
  102.7 46.4 %second_layer.1 = f32[1024,512]{1,0:T(8,128)} custom-call(s32[16]{0:T(128)} %select_reduce_fusion.refs_0_, f32[4,4,5,64,128]{4,3,2,1,0:T(8,128)} %bitcast.37, f32[1,512]{1,0:T(1,128)} %get-tuple-element.50.refs_2_, f32[1,512]{1,0:T(1,128)} %get-tuple-element.35.refs_3_, f32[2,3,512,128]{3,2,1,0:T(8,128)} %refs_4_.3, f32[2,128,512]{2,1,0:T(8,128)} %refs_5_.3, ...), custom_call_target="tpu_custom_call" | custom-call | tf_op jit(solution)/shard_map/second_layer/pallas_call | solution.py:840
  149.3 0.1 select_n.51
  149.7 5.1 %fusion = f32[960,512]{1,0:T(8,128)} fusion(f32[1024,512]{1,0:T(8,128)} %second_layer.1, s32[1024]{0:T(1024)S(1)} %copy-done.2, s32[960]{0:T(1024)S(1)} %pad_add_fusion), kind=kOutput, calls=%fused_computation | convolution fusion | flops 3020881920 | bytes 4071168 | tf_op jit(solution)/shard_map/dot_general | solution.py:140
  154.8 23.3 %scatter.1 = f32[240,512]{1,0:T(8,128)} custom-call(f32[4,240,512]{2,1,0:T(8,128)} %bitcast.40), custom_call_target="tpu_custom_call" | custom-call | tf_op jit(solution)/shard_map/scatter/pallas_call | solution.py:294
  178.1 1.1 reshape.244
  179.3 1.1 multiply_reduce_fusion.1
  180.5 0.1 multiply_multiply_fusion
  180.7 3.0 %fusion.4 = f32[10,18,1024]{2,1,0:T(8,128)S(1)} fusion(f32[2,512,1024]{2,1,0:T(8,128)} %param.24, f32[12,20,512]{2,1,0:T(8,128)S(1)} %multiply_multiply_fusion, f32[512]{0:T(512)S(1)} %bitcast.44, f32[512]{0:T(512)S(1)} %bitcast.45, f32[512]{0:T(512)S(1)} %bitcast.46, f32[512]{0:T(512)S(1)} %bitcast.47, f32[512]{0:T(512)S(1)} %bitcast.48, ...), kind=kOutput, calls=%fused_computation.4 | convolution fusion | flops 567797760 | bytes 7276544 | tf_op jit(solution)/shard_map/dot_general | solution.py:140
  183.8 0.3 multiply_reduce_fusion
  184.2 0.1 multiply_multiply_fusion.1
  184.3 2.5 %fusion.2 = f32[8,16,1024]{2,1,0:T(8,128)S(1)} fusion(f32[2,512,1024]{2,1,0:T(8,128)} %param.24, f32[10,18,512]{2,1,0:T(8,128)S(1)} %multiply_multiply_fusion.1, f32[512]{0:T(512)S(1)} %bitcast.53, f32[512]{0:T(512)S(1)} %bitcast.54, f32[512]{0:T(512)S(1)} %bitcast.55, f32[512]{0:T(512)S(1)} %bitcast.56, f32[512]{0:T(512)S(1)} %bitcast.57, ...), kind=kOutput, calls=%fused_computation.2 | convolution fusion | flops 403767296 | bytes 4999168 | tf_op jit(solution)/shard_map/dot_general | solution.py:140
  186.8 0.8 fusion.36
  (29 shorter events, 0.7 us)
Async XLA Ops:
  102.7 47.0 %copy-start.2 = (s32[1024]{0:T(1024)S(1)}, s32[1024]{0:T(1024)}, u32[]{:S(2)}) copy-start(s32[1024]{0:T(1024)} %param.22) | copy-start | bytes 12292
  154.8 24.4 %copy-start.1 = (f32[2,512]{1,0:T(2,128)S(1)}, f32[2,512]{1,0:T(2,128)}, u32[]{:S(2)}) copy-start(f32[2,512]{1,0:T(2,128)} %param.25) | copy-start | bytes 12292
  154.8 25.8 %copy-start = (f32[2,3,3,512]{3,0,2,1:T(2,128)S(1)}, f32[2,3,3,512]{3,0,2,1:T(2,128)}, u32[]{:S(2)}) copy-start(f32[2,3,3,512]{3,0,2,1:T(2,128)} %param.23) | copy-start | bytes 110596

commit v2 on v0

--- a/solution.py
+++ b/solution.py
@@ -546,6 +546,609 @@
     )(stream, mlp_gain[layer][None, :], w_up[layer], w_down[layer])
 
 
+def gelu(values):
+    return 0.5 * values * (1.0 + lax.erf(values * (0.5**0.5)))
+
+
+def piece(i, size):
+    return pl.ds(pl.multiple_of(i * size, size), size)
+
+
+class Layer:
+    def __init__(self, layer, refs, heads, chunk, kinds):
+        self.__dict__.update(refs)
+        self.layer, self.heads, self.chunk, self.kinds = layer, heads, chunk, kinds
+        self.cols, self.reps, self.c, self.r = position()
+        self.ntok, self.t = lax.axis_size("tok"), lax.axis_index("tok")
+        self.me = self.c * self.reps + self.r
+        self.mate, self.peer = {"rep": 1 - self.r}, {"col": 1 - self.c}
+        self.peers = [{"tok": lax.rem(self.t + e, self.ntok)} for e in range(1, self.ntok)]
+        self.rows, self.width = self.a_s.shape
+        self.lanes = self.q_s.shape[-1] // 2
+        self.n = self.rows // chunk
+        self.started = []
+
+    def sent(self, kind, i, src, dst, device):
+        k = self.kinds.index(kind)
+        return remote(src, dst, self.sem.at[k, 0, i], self.sem.at[k, 1, i], device)
+
+    def load_weights(self):
+        pairs = (
+            (self.wqkv_ref, self.wqkv_f), (self.wo_ref, self.wo_f),
+            (self.wu_ref, self.wu_f), (self.wd_ref, self.wd_f),
+        )
+        self.loads = [
+            pltpu.make_async_copy(src.at[self.layer], dst, self.wsem.at[j])
+            for j, (src, dst) in enumerate(pairs)
+        ]
+        for load in self.loads:
+            load.start()
+
+    def split_weights(self):
+        self.loads[0].wait()
+        for m in range(3):
+            self.wqkv_s[0, m], self.wqkv_s[1, m] = split(self.wqkv_f[m])
+        rest = ((self.wo_f, self.wo_s), (self.wu_f, self.wu_s), (self.wd_f, self.wd_s))
+        for load, (src, dst) in zip(self.loads[1:], rest):
+            load.wait()
+            dst[0], dst[1] = split(src[...])
+
+    def project(self, stream):
+        normed = split(layer_norm(stream, self.ga_ref[pl.ds(self.layer, 1)]))
+        return [dot3(normed, (self.wqkv_s[0, m], self.wqkv_s[1, m])) for m in range(3)]
+
+    def pack(self, at, q, k, v):
+        lanes, heads = self.lanes, self.heads
+        half_lanes, half_heads = lanes // 2, heads // 2
+        lane = lax.broadcasted_iota(jnp.int32, (1, lanes), 1)
+        low = lane < half_lanes
+        qh, ql = split(q * (HD ** (-0.5) * math.log2(math.e)))
+        kh, kl = [part.astype(jnp.float32) for part in split(k)]
+        vh, vl = [part.astype(jnp.float32) for part in split(v)]
+        qf, qlf = qh.astype(jnp.float32), ql.astype(jnp.float32)
+        q_s, k_s, v_s = self.q_s, self.k_s, self.v_s
+        q_s[0, at, :lanes] = qh
+        q_s[1, at, :lanes] = qh
+        q_s[0, at, lanes:] = jnp.where(low, qf, pltpu.roll(qlf, half_lanes, 1)).astype(jnp.bfloat16)
+        q_s[1, at, lanes:] = jnp.where(low, pltpu.roll(qf, half_lanes, 1), qlf).astype(jnp.bfloat16)
+        kh_r, kl_r = pltpu.roll(kh, half_lanes, 1), pltpu.roll(kl, half_lanes, 1)
+        for h in range(heads):
+            own = lane // HD == h
+            other = lane // HD == (h + half_heads) % heads
+            k_s[h, at, :lanes] = jnp.where(own, kh, 0.0).astype(jnp.bfloat16)
+            if h < half_heads:
+                mixed = jnp.where(own, kl, jnp.where(other, kh_r, 0.0))
+            else:
+                mixed = jnp.where(own, kh, jnp.where(other, kl_r, 0.0))
+            k_s[h, at, lanes:] = mixed.astype(jnp.bfloat16)
+            v_s[h, at, :lanes] = jnp.where(own, vh, 0.0).astype(jnp.bfloat16)
+            v_s[h, at, lanes:] = jnp.where(own, vl, 1.0).astype(jnp.bfloat16)
+
+    def near(self, i):
+        half = self.chunk // 2
+        start = pl.multiple_of(i * self.chunk + (1 - self.r) * half, half)
+        return self.sent("near", i, self.p_s.at[pl.ds(start, half)], self.n1_s.at[piece(i, half)], self.mate)
+
+    def far(self, i):
+        at = piece(i, self.chunk // 2)
+        return self.sent("far", i, self.s1_s.at[at], self.f1_s.at[at], self.peer)
+
+    def own_half(self, i):
+        half = self.chunk // 2
+        return pl.ds(pl.multiple_of(i * self.chunk + self.r * half, half), half)
+
+    def share(self, i):
+        at = self.own_half(i)
+        return self.sent("share", i, self.a_s.at[at], self.a_s.at[at], self.mate)
+
+    def attention(self, k):
+        lanes, half_heads = self.lanes, self.heads // 2
+        lane = lax.broadcasted_iota(jnp.int32, (1, lanes), 1)
+        i, half = k // 2, k % 2
+        at = piece(i, self.chunk)
+        total = jnp.zeros((self.chunk, lanes), jnp.float32)
+        for m in range(half_heads):
+            h = half * half_heads + m
+            scores = bdot(self.q_s[half, at, :], self.k_s[h], (((1,), (1,)), ((), ())))
+            weights = jnp.exp2(scores - jnp.max(scores, axis=-1, keepdims=True))
+            wh, wl = split(weights)
+            sums = bdot(wh, self.v_s[h]) + bdot(wl, self.v_s[h])
+            top, low = sums[:, :lanes], sums[:, lanes:]
+            total += jnp.where(lane // HD == h, (top + low) / pltpu.roll(low, lanes // 2, 1), 0.0)
+        self.att_s[half] = total
+
+    def finish(self, i):
+        projection = (self.wo_s[0], self.wo_s[1])
+        self.p_s[piece(i, self.chunk)] = dot3(split(self.att_s[0] + self.att_s[1]), projection)
+        self.near(i).start()
+
+    def reduce_near(self, i):
+        self.near(i).wait_recv()
+        at = piece(i, self.chunk // 2)
+        self.s1_s[at] = self.p_s[self.own_half(i)] + self.n1_s[at]
+        self.far(i).start()
+
+    def reduce_far(self, i):
+        self.far(i).wait_recv()
+        half = self.chunk // 2
+        at = piece(i, half)
+        stream = self.stream_rows(i * self.chunk + self.r * half, half)
+        self.a_s[self.own_half(i)] = (self.s1_s[at] + self.f1_s[at]) + stream
+        self.share(i).start()
+
+    def mlp(self, x):
+        normed = split(layer_norm(x, self.gm_ref[pl.ds(self.layer, 1)]))
+        hidden = gelu(dot3(normed, (self.wu_s[0], self.wu_s[1])))
+        return dot3(split(hidden), (self.wd_s[0], self.wd_s[1]))
+
+    def run(self, stages):
+        n = self.n
+
+        def tick(k, carry):
+            @pl.when(k < 2 * n)
+            def _():
+                self.attention(k)
+
+            for offset, stage in stages:
+                @pl.when((k >= offset) & (k < offset + 2 * n) & ((k - offset) % 2 == 0))
+                def _(offset=offset, stage=stage):
+                    stage((k - offset) // 2)
+
+            return carry
+
+        lax.fori_loop(0, 2 * n + stages[0][0] - 1, tick, 0)
+
+
+class First(Layer):
+    def stream_rows(self, start, count):
+        at = pl.ds(pl.multiple_of(start, count), count)
+        return jnp.concatenate([self.g_s[j, at] for j in range(self.cols * self.reps)], axis=-1)
+
+    def across(self, i):
+        at = piece(i, self.chunk)
+        return self.sent("across", i, self.x_ref.at[at], self.g_s.at[self.me, at], self.peer)
+
+    def over(self, i):
+        at = piece(i, self.chunk)
+        return self.sent("over", i, self.x_ref.at[at], self.g_s.at[self.me, at], self.mate)
+
+    def relay(self, i):
+        at = piece(i, self.chunk)
+        slot = (1 - self.c) * self.reps + self.r
+        return self.sent("relay", i, self.g_s.at[slot, at], self.g_s.at[slot, at], self.mate)
+
+    def code(self, e):
+        target = lax.rem(self.t + e, self.ntok)
+        return self.sent(
+            "code", e, self.code_ref.at[target], self.arrived_ref.at[self.t], {"tok": target}
+        )
+
+    def near2(self, i):
+        at = piece(i, self.chunk)
+        return self.sent("near2", i, self.m_s.at[1 - self.r, :, at], self.n2_s.at[:, at], self.mate)
+
+    def far2(self, i):
+        at = piece(i, self.chunk)
+        return self.sent("far2", i, self.s2_s.at[at], self.f2_s.at[at], self.peer)
+
+    def feed(self, i):
+        self.share(i).wait_recv()
+        at = piece(i, self.chunk)
+        total = self.mlp(self.a_s[at])
+        for j in range(self.cols * self.reps):
+            self.m_s[j % self.reps, j // self.reps, at] = total[:, j * self.lanes : (j + 1) * self.lanes]
+        self.near2(i).start()
+
+    def scatter_near(self, i):
+        self.near2(i).wait_recv()
+        at = piece(i, self.chunk)
+        self.s2_s[at] = self.m_s[self.r, 1 - self.c, at] + self.n2_s[1 - self.c, at]
+        self.far2(i).start()
+
+    def scatter_far(self, i):
+        self.far2(i).wait_recv()
+        at = piece(i, self.chunk)
+        own = self.a_s[at, piece(self.me, self.lanes)]
+        total = (self.m_s[self.r, self.c, at] + self.n2_s[self.c, at]) + self.f2_s[at]
+        self.out_ref[at] = total + own
+
+    def body(self):
+        n = self.n
+        self.load_weights()
+        greet([self.mate, self.peer] + self.peers)
+        for i in range(n):
+            self.across(i).start()
+        for i in range(n):
+            self.over(i).start()
+        for e in range(1, self.ntok):
+            self.code(e).start()
+        self.arrived_ref[self.t] = self.code_ref[self.t]
+        self.g_s[self.me] = self.x_ref[...]
+        self.split_weights()
+
+        def step(i, carry):
+            @pl.when(i < n)
+            def _():
+                self.across(i).wait_recv()
+                self.relay(i).start()
+
+            @pl.when(i > 0)
+            def _():
+                self.over(i - 1).wait_recv()
+                self.relay(i - 1).wait_recv()
+                stream = self.stream_rows((i - 1) * self.chunk, self.chunk)
+                self.pack(piece(i - 1, self.chunk), *self.project(stream))
+
+            return carry
+
+        lax.fori_loop(0, n + 1, step, 0)
+        self.run(
+            [
+                (9, self.scatter_far), (7, self.scatter_near), (6, self.feed),
+                (5, self.reduce_far), (2, self.reduce_near), (1, self.finish),
+            ]
+        )
+        for copy in (
+            self.near, self.far, self.share, self.near2, self.far2, self.across, self.over, self.relay
+        ):
+            for i in range(n):
+                copy(i).wait_send()
+        for e in range(1, self.ntok):
+            self.code(e).wait()
+
+
+class Second(Layer):
+    def stream_rows(self, start, count):
+        parts = []
+        for m in range(count // self.block):
+            at = self.source_ref[start // self.block + m]
+            places = [self.g_s[at // self.cap, j, at % self.cap] for j in range(self.cols * self.reps)]
+            parts.append(jnp.concatenate(places, axis=-1))
+        return jnp.concatenate(parts, axis=0)
+
+    def along(self, e, j):
+        target = lax.rem(self.t + e, self.ntok)
+        return self.sent(
+            "along", e * self.cap + j, self.o_s.at[target, j], self.g_s.at[self.t, self.me, j],
+            {"tok": target},
+        )
+
+    def origin(self, e):
+        return lax.rem(self.t + self.ntok - e, self.ntok)
+
+    def placed(self, kind, e, j, slot, device):
+        ref = self.g_s.at[self.origin(e), slot, j]
+        return self.sent(kind, e * self.cap + j, ref, ref, device)
+
+    def across(self, e, j):
+        return self.placed("across", e, j, self.me, self.peer)
+
+    def over(self, e, j):
+        return self.placed("over", e, j, self.me, self.mate)
+
+    def relay(self, e, j):
+        return self.placed("relay", e, j, (1 - self.c) * self.reps + self.r, self.mate)
+
+    def arrive(self, e):
+        for j in range(self.cap):
+            if e:
+                self.along(e, j).wait_recv()
+            self.across(e, j).start()
+            self.over(e, j).start()
+
+    def hand(self, e):
+        for j in range(self.cap):
+            self.across(e, j).wait_recv()
+            self.relay(e, j).start()
+
+    def take(self, e):
+        for j in range(self.cap):
+            self.over(e, j).wait_recv()
+            self.relay(e, j).wait_recv()
+        u = self.origin(e)
+        parts = []
+        for j in range(self.cap):
+            places = [self.g_s[u, k, j] for k in range(self.cols * self.reps)]
+            parts.append(jnp.concatenate(places, axis=-1))
+        for m, values in enumerate(self.project(jnp.concatenate(parts, axis=0))):
+            for j in range(self.cap):
+                self.raw_s[m, u * self.cap + j] = values[j * self.block : (j + 1) * self.block]
+
+    def move(self):
+        for u in range(self.ntok):
+            for j in range(self.cap):
+                self.o_s[u, j] = self.x_ref[self.index_ref[u * self.cap + j]]
+        for j in range(self.cap):
+            self.g_s[self.t, self.me, j] = self.x_ref[self.index_ref[self.t * self.cap + j]]
+        order = [0]
+        for e in range(1, self.ntok // 2 + 1):
+            order += [e] + ([self.ntok - e] if self.ntok - e != e else [])
+        for j in range(self.cap):
+            for e in order[1:]:
+                self.along(e, j).start()
+        self.arrive(0)
+        self.split_weights()
+        self.split_points()
+        for at, e in enumerate(order[1:]):
+            self.arrive(e)
+            self.hand(order[at])
+            if at:
+                self.take(order[at - 1])
+        self.hand(order[-1])
+        for e in order[-2:]:
+            self.take(e)
+
+        def step(i, carry):
+            def row(m):
+                each = self.chunk // self.block
+                blocks = [self.raw_s[m, self.source_ref[i * each + k]] for k in range(each)]
+                return jnp.concatenate(blocks, axis=0)
+
+            self.pack(piece(i, self.chunk), row(0), row(1), row(2))
+            return carry
+
+        lax.fori_loop(0, self.n, step, 0)
+
+    def load_points(self):
+        self.point = pltpu.make_async_copy(self.pw_ref, self.pw_f, self.wsem.at[4])
+        self.point.start()
+
+    def split_points(self):
+        self.point.wait()
+
+        def step(k, carry):
+            at = piece(k, 64)
+            for l in range(2):
+                self.pw_s[0, l, at], self.pw_s[1, l, at] = split(self.pw_f[l, at])
+            return carry
+
+        lax.fori_loop(0, self.width // 64, step, 0)
+
+    def cell_ids(self):
+        count = self.pool_s.shape[0]
+        p = lax.broadcasted_iota(jnp.int32, (count, 1), 0)
+        wide = TC + 2 * HALO
+        row = ((p.astype(jnp.float32) + 0.5) * (1.0 / wide)).astype(jnp.int32)
+        col = row // TR
+        x = col * TC - HALO + (p - row * wide)
+        full = TC * self.cols
+        y = row - col * TR
+        return jnp.where((x >= 0) & (x < full), (self.t * TR + y) * full + x, -2)
+
+    def feed(self, i):
+        self.share(i).wait_recv()
+        at = piece(i, self.chunk)
+        x = self.a_s[at]
+        high, low = split(self.mlp(x) + x * (1.0 / (self.cols * self.reps)))
+        chosen = jnp.where(self.cell_ids() == self.pillar_ref[:, at], 1.0, 0.0).astype(jnp.bfloat16)
+        self.pool_s[...] += bdot(chosen, high) + bdot(chosen, low)
+
+    def tile_part(self, c, r, k):
+        cells = self.pool_s.shape[0] // (self.cols * self.reps)
+        start = (c * self.reps + r) * cells + k * self.edge
+        return pl.ds(pl.multiple_of(start, 8), self.edge)
+
+    def near3(self, w, k):
+        c = self.c if w else 1 - self.c
+        return self.sent(
+            "near3", w * self.pieces + k, self.pool_s.at[self.tile_part(c, 1 - self.r, k)],
+            self.n3_s.at[w, k], self.mate,
+        )
+
+    def far3(self, k):
+        return self.sent("far3", k, self.s3_s.at[k], self.f3_s.at[k], self.peer)
+
+    def inner(self):
+        start = jnp.where(self.r == 0, self.pieces * self.edge, self.edge)
+        src = self.tile_s.at[pl.ds(pl.multiple_of(start, 8), self.edge)]
+        return self.sent("halo", 0, src, self.h_s.at[0], self.mate)
+
+    def outer(self):
+        start = jnp.where(self.r == 0, self.edge, self.pieces * self.edge)
+        src = self.tile_s.at[pl.ds(pl.multiple_of(start, 8), self.edge)]
+        return self.sent("halo", 1, src, self.h_s.at[1], self.partner)
+
+    def scatter(self):
+        order = [0, self.pieces - 1] + list(range(1, self.pieces - 1))
+        for w in range(2):
+            for k in order:
+                self.near3(w, k).start()
+        for k in order:
+            self.near3(0, k).wait_recv()
+            self.s3_s[k] = self.pool_s[self.tile_part(1 - self.c, self.r, k)] + self.n3_s[0, k]
+            self.far3(k).start()
+        for at, k in enumerate(order):
+            self.near3(1, k).wait_recv()
+            self.far3(k).wait_recv()
+            own = self.pool_s[self.tile_part(self.c, self.r, k)] + self.n3_s[1, k]
+            self.tile_s[pl.ds((k + 1) * self.edge, self.edge)] = own + self.f3_s[k]
+            if at == 1:
+                self.inner().start()
+                self.outer().start()
+        self.inner().wait()
+        self.outer().wait()
+        wrapped = jnp.where(self.r == 0, self.t == 0, self.t == self.ntok - 1)
+        beyond = jnp.where(wrapped, 0.0, self.h_s[1])
+        within = self.h_s[0]
+        self.tile_s[: self.edge] = jnp.where(self.r == 0, beyond, within)
+        self.tile_s[(self.pieces + 1) * self.edge :] = jnp.where(self.r == 0, within, beyond)
+
+    def raster(self):
+        wide = TC + 2 * HALO
+        rows = self.tile_s.shape[0] // wide
+        pad = (self.flat_s.shape[0] - rows * wide) // 2
+        self.flat_s[:pad] = jnp.zeros((pad, self.width), jnp.float32)
+        self.flat_s[pad + rows * wide :] = jnp.zeros((pad, self.width), jnp.float32)
+        for l in range(2):
+            old = pl.ds(l * wide, (rows - 2 * l) * wide)
+            start, count = (l + 1) * wide, (rows - 2 * l - 2) * wide
+            cells = self.tile_s[old]
+            square = jnp.mean(cells * cells, axis=-1, keepdims=True)
+            gain = self.rg_ref[pl.ds(l, 1)]
+            self.flat_s[pl.ds(pad + l * wide, (rows - 2 * l) * wide)] = (
+                cells * lax.rsqrt(square + EPSILON) * gain
+            )
+            mixed = jnp.zeros((count, self.width), jnp.float32)
+            for a in range(3):
+                for b in range(3):
+                    shift = pad + start + (a - 1) * wide + b - 1
+                    mixed = mixed + self.flat_s[pl.ds(shift, count)] * self.dw_ref[l, a, pl.ds(b, 1)]
+            both = dot3(split(mixed), (self.pw_s[0, l], self.pw_s[1, l]))
+            centre = self.tile_s[pl.ds(start, count)]
+            result = centre + both[:, : self.width] * jax.nn.sigmoid(both[:, self.width :])
+            if l == 0:
+                p = lax.broadcasted_iota(jnp.int32, (count, 1), 0) + start
+                row = ((p.astype(jnp.float32) + 0.5) * (1.0 / wide)).astype(jnp.int32)
+                y = (self.t * self.reps + self.r) * (rows - 2 * HALO) - HALO + row
+                x = self.c * TC - HALO + (p - row * wide)
+                inside = (y >= 0) & (y < TR * self.ntok) & (x >= 0) & (x < TC * self.cols)
+                result = jnp.where(inside, result, 0.0)
+            self.tile_s[pl.ds(start, count)] = result
+        for y in range(rows - 2 * HALO):
+            self.out_ref[y] = self.tile_s[pl.ds((y + HALO) * wide + HALO, TC)]
+
+    def body(self):
+        self.block = self.x_ref.shape[1]
+        self.cap = self.g_s.shape[2]
+        self.pieces, self.edge = self.s3_s.shape[:2]
+        step = jnp.where(self.r == 0, self.ntok - 1, 1)
+        self.partner = {"tok": lax.rem(self.t + step, self.ntok), "rep": 1 - self.r}
+        self.load_weights()
+        self.load_points()
+        greet([self.mate, self.peer, self.partner] + self.peers)
+        self.move()
+        self.pool_s[...] = jnp.zeros(self.pool_s.shape, jnp.float32)
+        self.run([(6, self.feed), (5, self.reduce_far), (2, self.reduce_near), (1, self.finish)])
+        self.scatter()
+        self.raster()
+        for copy in (self.near, self.far, self.share):
+            for i in range(self.n):
+                copy(i).wait_send()
+        for j in range(self.cap):
+            for e in range(self.ntok):
+                if e:
+                    self.along(e, j).wait_send()
+                for copy in (self.across, self.over, self.relay):
+                    copy(e, j).wait_send()
+        for k in range(self.pieces):
+            self.near3(0, k).wait_send()
+            self.near3(1, k).wait_send()
+            self.far3(k).wait_send()
+
+
+def run_layer(kind, layer, inputs, outputs, weights, collective_id, extra, kinds, most):
+    w_qkv, w_out, w_up, w_down, attn_gain, mlp_gain = weights
+    lanes, width, hidden = w_qkv.shape[-1], w_qkv.shape[-2], w_up.shape[-1]
+    heads, rows = lanes // HD, PATCH
+    chunk = min(256, rows)
+    dma, f32, b16 = pltpu.SemaphoreType.DMA, jnp.float32, jnp.bfloat16
+    vmem = pl.BlockSpec(memory_space=pltpu.VMEM)
+    hbm = pl.BlockSpec(memory_space=pl.ANY)
+    smem = pl.BlockSpec(memory_space=pltpu.SMEM)
+    inputs = dict(inputs)
+    places = {name: vmem for name in inputs}
+    inputs.update(ga_ref=attn_gain, gm_ref=mlp_gain)
+    inputs.update(wqkv_ref=w_qkv, wo_ref=w_out, wu_ref=w_up, wd_ref=w_down)
+    for name in ("index_ref", "source_ref"):
+        places[name] = smem
+    for name in ("wqkv_ref", "wo_ref", "wu_ref", "wd_ref", "pw_ref"):
+        places[name] = hbm
+    scratch = dict(
+        wqkv_f=pltpu.VMEM((3, width, lanes), f32),
+        wo_f=pltpu.VMEM((lanes, width), f32),
+        wu_f=pltpu.VMEM((width, hidden), f32),
+        wd_f=pltpu.VMEM((hidden, width), f32),
+        wqkv_s=pltpu.VMEM((2, 3, width, lanes), b16),
+        wo_s=pltpu.VMEM((2, lanes, width), b16),
+        wu_s=pltpu.VMEM((2, width, hidden), b16),
+        wd_s=pltpu.VMEM((2, hidden, width), b16),
+        q_s=pltpu.VMEM((2, rows, 2 * lanes), b16),
+        k_s=pltpu.VMEM((heads, rows, 2 * lanes), b16),
+        v_s=pltpu.VMEM((heads, rows, 2 * lanes), b16),
+        att_s=pltpu.VMEM((2, chunk, lanes), f32),
+        p_s=pltpu.VMEM((rows, width), f32),
+        n1_s=pltpu.VMEM((rows // 2, width), f32),
+        s1_s=pltpu.VMEM((rows // 2, width), f32),
+        f1_s=pltpu.VMEM((rows // 2, width), f32),
+        a_s=pltpu.VMEM((rows, width), f32),
+        sem=dma((len(kinds), 2, max(most, rows // chunk))),
+        wsem=dma((5,)),
+    )
+    scratch.update(extra)
+    names = list(inputs) + list(outputs) + list(scratch)
+
+    def kernel(*refs):
+        kind(layer, dict(zip(names, refs)), heads, chunk, kinds).body()
+
+    return pl.pallas_call(
+        kernel,
+        out_shape=tuple(outputs.values()),
+        in_specs=[places.get(name, vmem) for name in inputs],
+        out_specs=tuple(vmem for _ in outputs),
+        scratch_shapes=list(scratch.values()),
+        compiler_params=pltpu.CompilerParams(
+            collective_id=collective_id, has_side_effects=True, vmem_limit_bytes=VMEM_LIMIT
+        ),
+        name=kind.__name__.lower(),
+    )(*inputs.values())
+
+
+def first_layer(tokens, codes, weights, collective_id):
+    rows, lanes = tokens.shape
+    cols, reps = lax.axis_size("col"), lax.axis_size("rep")
+    f32 = jnp.float32
+    extra = dict(
+        g_s=pltpu.VMEM((cols * reps, rows, lanes), f32),
+        m_s=pltpu.VMEM((reps, cols, rows, lanes), f32),
+        n2_s=pltpu.VMEM((cols, rows, lanes), f32),
+        s2_s=pltpu.VMEM((rows, lanes), f32),
+        f2_s=pltpu.VMEM((rows, lanes), f32),
+    )
+    kinds = ("near", "far", "share", "near2", "far2", "across", "over", "relay", "code")
+    outputs = dict(
+        out_ref=jax.ShapeDtypeStruct((rows, lanes), f32),
+        arrived_ref=jax.ShapeDtypeStruct(codes.shape, codes.dtype),
+    )
+    inputs = dict(x_ref=tokens, code_ref=codes)
+    return run_layer(First, 0, inputs, outputs, weights, collective_id, extra, kinds, lax.axis_size("tok"))
+
+
+def second_layer(share, index, source, pillar, raster_weights, weights, collective_id):
+    cols, reps, ntok = lax.axis_size("col"), lax.axis_size("rep"), lax.axis_size("tok")
+    count, block, lanes = share.shape
+    cap = index.shape[0] // ntok
+    depth_weight, point_weight, raster_gain = raster_weights
+    width = depth_weight.shape[-1]
+    wide, rep_rows = TC + 2 * HALO, TR // reps
+    edge, pieces = HALO * wide, rep_rows // HALO
+    tile = (rep_rows + 2 * HALO) * wide
+    f32 = jnp.float32
+    extra = dict(
+        o_s=pltpu.VMEM((ntok, cap, block, lanes), f32),
+        g_s=pltpu.VMEM((ntok, cols * reps, cap, block, lanes), f32),
+        raw_s=pltpu.VMEM((3, ntok * cap, block, lanes), f32),
+        pw_f=pltpu.VMEM(point_weight.shape, f32),
+        pw_s=pltpu.VMEM((2,) + point_weight.shape, jnp.bfloat16),
+        pool_s=pltpu.VMEM((cols * reps * rep_rows * wide, width), f32),
+        n3_s=pltpu.VMEM((2, pieces, edge, width), f32),
+        s3_s=pltpu.VMEM((pieces, edge, width), f32),
+        f3_s=pltpu.VMEM((pieces, edge, width), f32),
+        h_s=pltpu.VMEM((2, edge, width), f32),
+        tile_s=pltpu.VMEM((tile, width), f32),
+        flat_s=pltpu.VMEM((tile + 16, width), f32),
+    )
+    kinds = ("near", "far", "share", "along", "across", "over", "relay", "near3", "far3", "halo")
+    outputs = dict(out_ref=jax.ShapeDtypeStruct((rep_rows, TC, width), f32))
+    inputs = dict(
+        index_ref=index, source_ref=source, x_ref=share, pillar_ref=pillar[None, :],
+        dw_ref=depth_weight, rg_ref=raster_gain, pw_ref=point_weight,
+    )
+    return run_layer(Second, 1, inputs, outputs, weights, collective_id, extra, kinds, ntok * cap)[0]
+
+
+HALO = 2
+
+
 def routes(dest_device, dest_slot):
     count = dest_device.shape[0]
     peers = lax.axis_size("tok")
@@ -559,6 +1162,12 @@
     code = jnp.pad(code.reshape(peers, capacity), ((0, 0), (0, 128 - capacity)))
     code = jnp.broadcast_to(code[:, None, :], (peers, 8, 128)).astype(jnp.float32)
     return index, code, capacity
+
+
+def places(arrived, capacity, order):
+    held = arrived[:, 0, :capacity].reshape(-1).astype(jnp.int32)
+    found = held[None, :] == order[:, None] + 1
+    return jnp.sum(jnp.where(found, jnp.arange(held.shape[0], dtype=jnp.int32)[None, :], 0), axis=1)
 
 
 def raster_cells(extended, depth_weight, point_weight, gain_row):
@@ -578,9 +1187,6 @@
     combined = combined.reshape(row_count, col_count, 2 * channels)
     centre = extended[1:-1, 1:-1]
     return centre + combined[..., :channels] * jax.nn.sigmoid(combined[..., channels:])
-
-
-HALO = 2
 
 
 def extended_cells(tok, members, rep_rows, full_width):
@@ -634,6 +1240,14 @@
     order = jnp.arange(block_count, dtype=jnp.int32)
     index, codes, capacity = routes(dest_device, dest_slot)
     width = tokens.shape[1]
+    weights = (w_qkv, w_out, w_up, w_down, attn_gain, mlp_gain)
+    whole = (2 * members[1] * HALO * (TC + 2 * HALO)) % 8 == 0 and TR % (members[1] * HALO) == 0
+    if members == (2, 2) and ntok > 1 and tokens.shape[0] == PATCH and whole:
+        share, arrived = first_layer(tokens, codes, weights, 1)
+        source = places(arrived, capacity, order)
+        share = share.reshape(block_count, -1, width)
+        raster_weights = (depth_weight, point_weight, raster_gain)
+        return second_layer(share, index, source, pillar, raster_weights, weights, 5)
     blocks = gather(tokens, 1).reshape(1, group, block_count, -1, width)
     stream = attention_layer(blocks, order, 0, w_qkv, w_out, attn_gain, 2)
     share = scatter(mlp_partial(stream, 0, w_up, w_down, mlp_gain, group), 3)
@@ -641,9 +1255,7 @@
     outgoing = outgoing.reshape(ntok, -1, width)
     moved, arrived = move(outgoing, codes, 4)
     blocks = moved.reshape(ntok, group, capacity, -1, width)
-    held = arrived[:, 0, :capacity].reshape(-1).astype(jnp.int32)
-    found = held[None, :] == order[:, None] + 1
-    source = jnp.sum(jnp.where(found, jnp.arange(held.shape[0], dtype=jnp.int32)[None, :], 0), axis=1)
+    source = places(arrived, capacity, order)
     stream = attention_layer(blocks, source, 1, w_qkv, w_out, attn_gain, 5)
     partial = mlp_partial(stream, 1, w_up, w_down, mlp_gain, 1)[0]
 

time: 251 us -> 164 us (0.65)
  Pallas kernels: 222 us -> 156 us
  matrix products: 10.6 us -> 0 us
  local copies, waits for them, and re-layouts: 11.7 us -> 3.84 us
    pallas_call x11 -> x2, Pallas kernels: 222 us -> 156 us  [run_layer(): pl.pallas_call(kernel, out_shape=tuple(outputs.values()), in_specs=[place...]
    dot_general x3 -> x0, matrix products: 10.6 us -> none  [matmul(): jnp.dot(left, right, precision=MATMUL_PRECISION, preferred_element_type=j...]
    unnamed x31 -> x2, local copies, waits for them, and re-layouts: 8.68 us -> 3.07 us
where the time goes in v2:
time: 164 us
  Pallas kernels  156 us (95%)
  local copies, waits for them, and re-layouts  3.84 us (2%)
  other arithmetic  3.67 us (2%)
    pallas_call x2, Pallas kernels, run_layer(): pl.pallas_call(kernel, out_shape=tuple(outputs.values()), in_specs=[place...  156 us

profile of v2, /device:TPU:0, one launch (start us, length us, event | category | flops | bytes accessed | tf_op | source)
XLA Modules:
  0.0 163.6 jit_solution(12563055896036949921)
XLA Ops:
  0.0 0.9 convert_reduce_fusion
  0.9 0.7 multiply_add_fusion
  1.6 0.7 select_reduce_fusion.1
  2.3 0.1 reshape.23
  2.3 0.6 broadcast_in_dim.53.refs_1_
  3.0 1.4 copy.15.refs_4_
  4.4 71.1 %first.1 = (f32[1024,128]{1,0:T(8,128)}, f32[4,8,128]{2,1,0:T(8,128)}) custom-call(f32[1024,128]{1,0:T(8,128)} %refs_0_.1, f32[4,8,128]{2,1,0:T(8,128)} %broadcast_in_dim.53.refs_1_, f32[2,512]{1,0:T(2,128)} %refs_7_.3, f32[2,512]{1,0:T(2,128)} %refs_8_.1, f32[2,3,512,128]{3,2,1,0:T(8,128)} %refs_9_.1, f32[2,128,512]{2,1,0:T(8,128)} %refs_10_.1, ...), custom_call_target="tpu_custom_call" | custom-call | tf_op jit(solution)/shard_map/first/pallas_call | solution.py:1083
  75.4 0.7 convert_reduce_fusion.1
  76.2 0.1 convert_element_type.19
  76.2 0.7 select_reduce_fusion.refs_1_
  76.9 85.0 %second.1 = f32[8,16,512]{2,1,0:T(8,128)} custom-call(s32[20]{0:T(128)} %get-tuple-element.10.refs_0_, s32[16]{0:T(128)} %select_reduce_fusion.refs_1_, f32[16,64,128]{2,1,0:T(8,128)} %bitcast.2, s32[1,1024]{1,0:T(1,128)} %bitcast.3, f32[2,3,3,512]{3,2,1,0:T(4,128)} %copy.15.refs_4_, f32[2,512]{1,0:T(2,128)} %refs_5_.3, f32[2,512,1024]{2,1,0:T(8,128)} %refs_6_.3, ...), custom_call_target="tpu_custom_call" | custom-call | tf_op jit(solution)/shard_map/second/pallas_call | solution.py:1083
  162.0 1.7 %copy.17 = f32[8,16,512]{2,1,0:T(8,128)} copy(f32[8,16,512]{2,1,0:T(8,128)} %second.1) | data formatting | bytes 524288
  (2 shorter events, 0.0 us)

commit v3 on v2

--- a/solution.py
+++ b/solution.py
@@ -598,8 +598,8 @@
         return [dot3(normed, (self.wqkv_s[0, m], self.wqkv_s[1, m])) for m in range(3)]
 
     def pack(self, at, q, k, v):
-        lanes, heads = self.lanes, self.heads
-        half_lanes, half_heads = lanes // 2, heads // 2
+        lanes = self.lanes
+        half_lanes = lanes // 2
         lane = lax.broadcasted_iota(jnp.int32, (1, lanes), 1)
         low = lane < half_lanes
         qh, ql = split(q * (HD ** (-0.5) * math.log2(math.e)))
@@ -607,22 +607,22 @@
         vh, vl = [part.astype(jnp.float32) for part in split(v)]
         qf, qlf = qh.astype(jnp.float32), ql.astype(jnp.float32)
         q_s, k_s, v_s = self.q_s, self.k_s, self.v_s
+
+        def roll(values):
+            return pltpu.roll(values, half_lanes, 1)
+
         q_s[0, at, :lanes] = qh
         q_s[1, at, :lanes] = qh
-        q_s[0, at, lanes:] = jnp.where(low, qf, pltpu.roll(qlf, half_lanes, 1)).astype(jnp.bfloat16)
-        q_s[1, at, lanes:] = jnp.where(low, pltpu.roll(qf, half_lanes, 1), qlf).astype(jnp.bfloat16)
-        kh_r, kl_r = pltpu.roll(kh, half_lanes, 1), pltpu.roll(kl, half_lanes, 1)
-        for h in range(heads):
-            own = lane // HD == h
-            other = lane // HD == (h + half_heads) % heads
-            k_s[h, at, :lanes] = jnp.where(own, kh, 0.0).astype(jnp.bfloat16)
-            if h < half_heads:
-                mixed = jnp.where(own, kl, jnp.where(other, kh_r, 0.0))
-            else:
-                mixed = jnp.where(own, kh, jnp.where(other, kl_r, 0.0))
-            k_s[h, at, lanes:] = mixed.astype(jnp.bfloat16)
-            v_s[h, at, :lanes] = jnp.where(own, vh, 0.0).astype(jnp.bfloat16)
-            v_s[h, at, lanes:] = jnp.where(own, vl, 1.0).astype(jnp.bfloat16)
+        q_s[0, at, lanes:] = jnp.where(low, qf, roll(qlf)).astype(jnp.bfloat16)
+        q_s[1, at, lanes:] = jnp.where(low, roll(qf), qlf).astype(jnp.bfloat16)
+        k_s[0, at, :lanes] = kh.astype(jnp.bfloat16)
+        k_s[1, at, :lanes] = kh.astype(jnp.bfloat16)
+        k_s[0, at, lanes:] = jnp.where(low, kl, roll(kh)).astype(jnp.bfloat16)
+        k_s[1, at, lanes:] = jnp.where(low, roll(kl), kh).astype(jnp.bfloat16)
+        v_s[0, at, :lanes] = vh.astype(jnp.bfloat16)
+        v_s[1, at, :lanes] = vh.astype(jnp.bfloat16)
+        v_s[0, at, lanes:] = jnp.where(low, vl, 1.0).astype(jnp.bfloat16)
+        v_s[1, at, lanes:] = jnp.where(low, 1.0, vl).astype(jnp.bfloat16)
 
     def near(self, i):
         half = self.chunk // 2
@@ -642,19 +642,28 @@
         return self.sent("share", i, self.a_s.at[at], self.a_s.at[at], self.mate)
 
     def attention(self, k):
-        lanes, half_heads = self.lanes, self.heads // 2
+        lanes, half_heads, chunk = self.lanes, self.heads // 2, self.chunk
+        wide = lax.broadcasted_iota(jnp.int32, (1, 2 * lanes), 1)
         lane = lax.broadcasted_iota(jnp.int32, (1, lanes), 1)
         i, half = k // 2, k % 2
-        at = piece(i, self.chunk)
-        total = jnp.zeros((self.chunk, lanes), jnp.float32)
+        query = self.q_s[half, piece(i, chunk), :]
+        queries = []
         for m in range(half_heads):
-            h = half * half_heads + m
-            scores = bdot(self.q_s[half, at, :], self.k_s[h], (((1,), (1,)), ((), ())))
-            weights = jnp.exp2(scores - jnp.max(scores, axis=-1, keepdims=True))
-            wh, wl = split(weights)
-            sums = bdot(wh, self.v_s[h]) + bdot(wl, self.v_s[h])
-            top, low = sums[:, :lanes], sums[:, lanes:]
-            total += jnp.where(lane // HD == h, (top + low) / pltpu.roll(low, lanes // 2, 1), 0.0)
+            first = (wide < lanes) & (wide // HD == half * half_heads + m)
+            second = (wide >= lanes) & ((wide % (lanes // 2)) // HD == m)
+            mask = jnp.where(first | second, 1.0, 0.0).astype(jnp.bfloat16)
+            queries.append(query * mask)
+        stacked = jnp.concatenate(queries, axis=0)
+        scores = bdot(stacked, self.k_s[half], (((1,), (1,)), ((), ())))
+        weights = jnp.exp2(scores - jnp.max(scores, axis=-1, keepdims=True))
+        sums = bdot(jnp.concatenate(split(weights), axis=0), self.v_s[half])
+        sums = sums[: half_heads * chunk] + sums[half_heads * chunk :]
+        total = jnp.zeros((chunk, lanes), jnp.float32)
+        for m in range(half_heads):
+            own = sums[m * chunk : (m + 1) * chunk]
+            top, low = own[:, :lanes], own[:, lanes:]
+            ratio = (top + low) / pltpu.roll(low, lanes // 2, 1)
+            total += jnp.where(lane // HD == half * half_heads + m, ratio, 0.0)
         self.att_s[half] = total
 
     def finish(self, i):
@@ -718,10 +727,43 @@
         return self.sent("relay", i, self.g_s.at[slot, at], self.g_s.at[slot, at], self.mate)
 
     def code(self, e):
-        target = lax.rem(self.t + e, self.ntok)
-        return self.sent(
-            "code", e, self.code_ref.at[target], self.arrived_ref.at[self.t], {"tok": target}
-        )
+        target = {"tok": lax.rem(self.t + e, self.ntok)}
+        return self.sent("code", e, self.code_s, self.arrived_s.at[self.t], target)
+
+    def route(self):
+        device = self.dd_ref[...].astype(jnp.float32)
+        slot = self.ds_ref[...].astype(jnp.float32)
+        count = device.shape[1]
+        row = lax.broadcasted_iota(jnp.int32, (count, count), 0)
+        col = lax.broadcasted_iota(jnp.int32, (count, count), 1)
+
+        def upright(values):
+            return jnp.sum(jnp.where(row == col, values, 0.0), axis=1, keepdims=True)
+
+        devices, slots = upright(device), upright(slot)
+        earlier = jnp.where((devices == device) & (col < row), 1.0, 0.0)
+        place = devices * self.cap + jnp.sum(earlier, axis=1, keepdims=True)
+        at = lax.broadcasted_iota(jnp.int32, (count, 128), 1).astype(jnp.float32)
+        block = lax.broadcasted_iota(jnp.int32, (count, 128), 0).astype(jnp.float32)
+        index = jnp.sum(jnp.where(place == at, block, 0.0), axis=0, keepdims=True)
+        code = jnp.sum(jnp.where(place == at, slots + 1.0, 0.0), axis=0, keepdims=True)
+        self.index_ref[...] = index.astype(jnp.int32)
+        self.code_s[...] = jnp.broadcast_to(code, self.code_s.shape)
+        self.arrived_s[self.t] = jnp.broadcast_to(code, self.code_s.shape)
+
+    def locate(self):
+        row = lax.broadcasted_iota(jnp.int32, (128, 128), 0)
+        col = lax.broadcasted_iota(jnp.int32, (128, 128), 1)
+        first = self.t * self.cap
+        valid = (row >= first) & (row < first + self.cap)
+        source = jnp.zeros((1, 128), jnp.float32)
+        for u in range(self.ntok):
+            codes = self.arrived_s[u][:1]
+            upright = jnp.sum(jnp.where(row == col, codes, 0.0), axis=1, keepdims=True)
+            found = valid & (upright == (col + 1).astype(jnp.float32))
+            entry = (row - first + u * self.cap).astype(jnp.float32)
+            source += jnp.sum(jnp.where(found, entry, 0.0), axis=0, keepdims=True)
+        self.source_ref[...] = source.astype(jnp.int32)
 
     def near2(self, i):
         at = piece(i, self.chunk)
@@ -760,11 +802,12 @@
             self.across(i).start()
         for i in range(n):
             self.over(i).start()
+        self.cap = capacity_of(self.dd_ref.shape[1], self.ntok)
+        self.route()
+        self.g_s[self.me] = self.x_ref[...]
+        self.split_weights()
         for e in range(1, self.ntok):
             self.code(e).start()
-        self.arrived_ref[self.t] = self.code_ref[self.t]
-        self.g_s[self.me] = self.x_ref[...]
-        self.split_weights()
 
         def step(i, carry):
             @pl.when(i < n)
@@ -795,13 +838,14 @@
                 copy(i).wait_send()
         for e in range(1, self.ntok):
             self.code(e).wait()
+        self.locate()
 
 
 class Second(Layer):
     def stream_rows(self, start, count):
         parts = []
         for m in range(count // self.block):
-            at = self.source_ref[start // self.block + m]
+            at = self.source_ref[0, start // self.block + m]
             places = [self.g_s[at // self.cap, j, at % self.cap] for j in range(self.cols * self.reps)]
             parts.append(jnp.concatenate(places, axis=-1))
         return jnp.concatenate(parts, axis=0)
@@ -829,59 +873,61 @@
     def relay(self, e, j):
         return self.placed("relay", e, j, (1 - self.c) * self.reps + self.r, self.mate)
 
-    def arrive(self, e):
-        for j in range(self.cap):
-            if e:
-                self.along(e, j).wait_recv()
+    def arrive(self, j):
+        for e in self.order[1:]:
+            self.along(e, j).wait_recv()
             self.across(e, j).start()
             self.over(e, j).start()
 
-    def hand(self, e):
-        for j in range(self.cap):
+    def hand(self, j):
+        for e in self.order:
             self.across(e, j).wait_recv()
             self.relay(e, j).start()
 
-    def take(self, e):
-        for j in range(self.cap):
+    def take(self, j):
+        parts = []
+        for e in self.order:
             self.over(e, j).wait_recv()
             self.relay(e, j).wait_recv()
-        u = self.origin(e)
-        parts = []
-        for j in range(self.cap):
-            places = [self.g_s[u, k, j] for k in range(self.cols * self.reps)]
+            places = [self.g_s[self.origin(e), k, j] for k in range(self.cols * self.reps)]
             parts.append(jnp.concatenate(places, axis=-1))
         for m, values in enumerate(self.project(jnp.concatenate(parts, axis=0))):
-            for j in range(self.cap):
-                self.raw_s[m, u * self.cap + j] = values[j * self.block : (j + 1) * self.block]
+            for at, e in enumerate(self.order):
+                entry = self.origin(e) * self.cap + j
+                self.raw_s[m, entry] = values[at * self.block : (at + 1) * self.block]
 
     def move(self):
+        self.order = [0]
+        for e in range(1, self.ntok // 2 + 1):
+            self.order += [e] + ([self.ntok - e] if self.ntok - e != e else [])
         for u in range(self.ntok):
             for j in range(self.cap):
-                self.o_s[u, j] = self.x_ref[self.index_ref[u * self.cap + j]]
+                self.o_s[u, j] = self.x_ref[self.index_ref[0, u * self.cap + j]]
         for j in range(self.cap):
-            self.g_s[self.t, self.me, j] = self.x_ref[self.index_ref[self.t * self.cap + j]]
-        order = [0]
-        for e in range(1, self.ntok // 2 + 1):
-            order += [e] + ([self.ntok - e] if self.ntok - e != e else [])
+            self.g_s[self.t, self.me, j] = self.x_ref[self.index_ref[0, self.t * self.cap + j]]
         for j in range(self.cap):
-            for e in order[1:]:
+            for e in self.order[1:]:
                 self.along(e, j).start()
-        self.arrive(0)
+        for j in range(self.cap):
+            self.across(0, j).start()
+            self.over(0, j).start()
         self.split_weights()
-        self.split_points()
-        for at, e in enumerate(order[1:]):
-            self.arrive(e)
-            self.hand(order[at])
-            if at:
-                self.take(order[at - 1])
-        self.hand(order[-1])
-        for e in order[-2:]:
-            self.take(e)
+        for j in range(self.cap):
+            self.arrive(j)
+            if j == 0:
+                self.split_points()
+            if j >= 1:
+                self.hand(j - 1)
+            if j >= 2:
+                self.take(j - 2)
+        self.hand(self.cap - 1)
+        for j in range(max(0, self.cap - 2), self.cap):
+            self.take(j)
 
         def step(i, carry):
             def row(m):
                 each = self.chunk // self.block
-                blocks = [self.raw_s[m, self.source_ref[i * each + k]] for k in range(each)]
+                blocks = [self.raw_s[m, self.source_ref[0, i * each + k]] for k in range(each)]
                 return jnp.concatenate(blocks, axis=0)
 
             self.pack(piece(i, self.chunk), row(0), row(1), row(2))
@@ -992,7 +1038,7 @@
             for a in range(3):
                 for b in range(3):
                     shift = pad + start + (a - 1) * wide + b - 1
-                    mixed = mixed + self.flat_s[pl.ds(shift, count)] * self.dw_ref[l, a, pl.ds(b, 1)]
+                    mixed = mixed + self.flat_s[pl.ds(shift, count)] * self.dw_ref[a, b, pl.ds(l, 1)]
             both = dot3(split(mixed), (self.pw_s[0, l], self.pw_s[1, l]))
             centre = self.tile_s[pl.ds(start, count)]
             result = centre + both[:, : self.width] * jax.nn.sigmoid(both[:, self.width :])
@@ -1050,7 +1096,8 @@
     inputs.update(ga_ref=attn_gain, gm_ref=mlp_gain)
     inputs.update(wqkv_ref=w_qkv, wo_ref=w_out, wu_ref=w_up, wd_ref=w_down)
     for name in ("index_ref", "source_ref"):
-        places[name] = smem
+        if name in inputs:
+            places[name] = smem
     for name in ("wqkv_ref", "wo_ref", "wu_ref", "wd_ref", "pw_ref"):
         places[name] = hbm
     scratch = dict(
@@ -1063,8 +1110,8 @@
         wu_s=pltpu.VMEM((2, width, hidden), b16),
         wd_s=pltpu.VMEM((2, hidden, width), b16),
         q_s=pltpu.VMEM((2, rows, 2 * lanes), b16),
-        k_s=pltpu.VMEM((heads, rows, 2 * lanes), b16),
-        v_s=pltpu.VMEM((heads, rows, 2 * lanes), b16),
+        k_s=pltpu.VMEM((2, rows, 2 * lanes), b16),
+        v_s=pltpu.VMEM((2, rows, 2 * lanes), b16),
         att_s=pltpu.VMEM((2, chunk, lanes), f32),
         p_s=pltpu.VMEM((rows, width), f32),
         n1_s=pltpu.VMEM((rows // 2, width), f32),
@@ -1093,9 +1140,13 @@
     )(*inputs.values())
 
 
-def first_layer(tokens, codes, weights, collective_id):
+def capacity_of(count, peers):
+    return max(2, (count + peers - 4) // (peers - 1))
+
+
+def first_layer(tokens, dest_device, dest_slot, weights, collective_id):
     rows, lanes = tokens.shape
-    cols, reps = lax.axis_size("col"), lax.axis_size("rep")
+    cols, reps, ntok = lax.axis_size("col"), lax.axis_size("rep"), lax.axis_size("tok")
     f32 = jnp.float32
     extra = dict(
         g_s=pltpu.VMEM((cols * reps, rows, lanes), f32),
@@ -1103,20 +1154,21 @@
         n2_s=pltpu.VMEM((cols, rows, lanes), f32),
         s2_s=pltpu.VMEM((rows, lanes), f32),
         f2_s=pltpu.VMEM((rows, lanes), f32),
+        code_s=pltpu.VMEM((8, 128), f32),
+        arrived_s=pltpu.VMEM((ntok, 8, 128), f32),
     )
     kinds = ("near", "far", "share", "near2", "far2", "across", "over", "relay", "code")
+    table = jax.ShapeDtypeStruct((1, 128), jnp.int32)
     outputs = dict(
-        out_ref=jax.ShapeDtypeStruct((rows, lanes), f32),
-        arrived_ref=jax.ShapeDtypeStruct(codes.shape, codes.dtype),
+        out_ref=jax.ShapeDtypeStruct((rows, lanes), f32), index_ref=table, source_ref=table
     )
-    inputs = dict(x_ref=tokens, code_ref=codes)
-    return run_layer(First, 0, inputs, outputs, weights, collective_id, extra, kinds, lax.axis_size("tok"))
-
-
-def second_layer(share, index, source, pillar, raster_weights, weights, collective_id):
+    inputs = dict(x_ref=tokens, dd_ref=dest_device[None, :], ds_ref=dest_slot[None, :])
+    return run_layer(First, 0, inputs, outputs, weights, collective_id, extra, kinds, ntok)
+
+
+def second_layer(share, index, source, cap, pillar, raster_weights, weights, collective_id):
     cols, reps, ntok = lax.axis_size("col"), lax.axis_size("rep"), lax.axis_size("tok")
     count, block, lanes = share.shape
-    cap = index.shape[0] // ntok
     depth_weight, point_weight, raster_gain = raster_weights
     width = depth_weight.shape[-1]
     wide, rep_rows = TC + 2 * HALO, TR // reps
@@ -1141,7 +1193,7 @@
     outputs = dict(out_ref=jax.ShapeDtypeStruct((rep_rows, TC, width), f32))
     inputs = dict(
         index_ref=index, source_ref=source, x_ref=share, pillar_ref=pillar[None, :],
-        dw_ref=depth_weight, rg_ref=raster_gain, pw_ref=point_weight,
+        dw_ref=jnp.transpose(depth_weight, (1, 2, 0, 3)), rg_ref=raster_gain, pw_ref=point_weight,
     )
     return run_layer(Second, 1, inputs, outputs, weights, collective_id, extra, kinds, ntok * cap)[0]
 
@@ -1152,7 +1204,7 @@
 def routes(dest_device, dest_slot):
     count = dest_device.shape[0]
     peers = lax.axis_size("tok")
-    capacity = max(2, (count + peers - 4) // (peers - 1))
+    capacity = capacity_of(count, peers)
     order = jnp.arange(count, dtype=jnp.int32)
     earlier = (dest_device[:, None] == dest_device[None, :]) & (order[None, :] < order[:, None])
     place = dest_device * capacity + jnp.sum(earlier.astype(jnp.int32), axis=1)
@@ -1242,12 +1294,11 @@
     width = tokens.shape[1]
     weights = (w_qkv, w_out, w_up, w_down, attn_gain, mlp_gain)
     whole = (2 * members[1] * HALO * (TC + 2 * HALO)) % 8 == 0 and TR % (members[1] * HALO) == 0
-    if members == (2, 2) and ntok > 1 and tokens.shape[0] == PATCH and whole:
-        share, arrived = first_layer(tokens, codes, weights, 1)
-        source = places(arrived, capacity, order)
+    if members == (2, 2) and ntok > 1 and tokens.shape[0] == PATCH and whole and ntok * capacity <= 128:
+        share, index, source = first_layer(tokens, dest_device, dest_slot, weights, 1)
         share = share.reshape(block_count, -1, width)
         raster_weights = (depth_weight, point_weight, raster_gain)
-        return second_layer(share, index, source, pillar, raster_weights, weights, 5)
+        return second_layer(share, index, source, capacity, pillar, raster_weights, weights, 5)
     blocks = gather(tokens, 1).reshape(1, group, block_count, -1, width)
     stream = attention_layer(blocks, order, 0, w_qkv, w_out, attn_gain, 2)
     share = scatter(mlp_partial(stream, 0, w_up, w_down, mlp_gain, group), 3)

time: 164 us -> 149 us (0.909)
  Pallas kernels: 156 us -> 147 us
  other arithmetic: 3.67 us -> 0 us
  local copies, waits for them, and re-layouts: 3.84 us -> 1.67 us
    pallas_call x2, Pallas kernels: 156 us -> 147 us  [run_layer(): pl.pallas_call(kernel, out_shape=tuple(outputs.values()), in_specs=[place...]
    reduce_sum x3 -> x0, other arithmetic: 2.24 us -> none  [the longest x1 0.91 us: routes(): place = dest_device * capacity + jnp.sum(earlier.astype(jnp.int32), axis=1)]
where the time goes in v3:
time: 149 us
  Pallas kernels  147 us (99%)
  local copies, waits for them, and re-layouts  1.67 us (1%)
    pallas_call x2, Pallas kernels, run_layer(): pl.pallas_call(kernel, out_shape=tuple(outputs.values()), in_specs=[place...  147 us

profile of v3, /device:TPU:0, one launch (start us, length us, event | category | flops | bytes accessed | tf_op | source)
XLA Modules:
  0.0 148.8 jit_solution(14234493640636472816)
XLA Ops:
  0.0 67.9 %first.1 = (f32[1024,128]{1,0:T(8,128)}, s32[1,128]{1,0:T(1,128)}, s32[1,128]{1,0:T(1,128)}) custom-call(f32[1024,128]{1,0:T(8,128)} %refs_0_.1, s32[1,16]{1,0:T(1,128)} %bitcast.8, s32[1,16]{1,0:T(1,128)} %bitcast.9, f32[2,512]{1,0:T(2,128)} %refs_7_.3, f32[2,512]{1,0:T(2,128)} %refs_8_.3, f32[2,3,512,128]{3,2,1,0:T(8,128)} %refs_9_.1, ...), custom_call_target="tpu_custom_call" | custom-call | tf_op jit(solution)/shard_map/first/pallas_call | solution.py:1130
  67.9 79.2 %second.1 = f32[8,16,512]{2,1,0:T(8,128)} custom-call(s32[1,128]{1,0:T(1,128)} %get-tuple-element.8.refs_0_, s32[1,128]{1,0:T(1,128)} %get-tuple-element.9.refs_1_, f32[16,64,128]{2,1,0:T(8,128)} %bitcast.5, s32[1,1024]{1,0:T(1,128)} %bitcast.7, f32[3,3,2,512]{3,2,1,0:T(2,128)} %bitcast.6, f32[2,512]{1,0:T(2,128)} %refs_5_.3, f32[2,512,1024]{2,1,0:T(8,128)} %refs_6_.3, ...), custom_call_target="tpu_custom_call" | custom-call | tf_op jit(solution)/shard_map/second/pallas_call | solution.py:1130
  147.1 1.7 %copy.15 = f32[8,16,512]{2,1,0:T(8,128)} copy(f32[8,16,512]{2,1,0:T(8,128)} %second.1) | data formatting | bytes 524288

commit v4 on v3

--- a/solution.py
+++ b/solution.py
@@ -705,7 +705,7 @@
 
             return carry
 
-        lax.fori_loop(0, 2 * n + stages[0][0] - 1, tick, 0)
+        lax.fori_loop(0, 2 * n + max(offset for offset, _ in stages) - 1, tick, 0)
 
 
 class First(Layer):
@@ -827,8 +827,8 @@
         lax.fori_loop(0, n + 1, step, 0)
         self.run(
             [
-                (9, self.scatter_far), (7, self.scatter_near), (6, self.feed),
-                (5, self.reduce_far), (2, self.reduce_near), (1, self.finish),
+                (1, self.finish), (2, self.reduce_near), (9, self.scatter_near),
+                (6, self.reduce_far), (7, self.feed), (13, self.scatter_far),
             ]
         )
         for copy in (
@@ -1064,7 +1064,7 @@
         greet([self.mate, self.peer, self.partner] + self.peers)
         self.move()
         self.pool_s[...] = jnp.zeros(self.pool_s.shape, jnp.float32)
-        self.run([(6, self.feed), (5, self.reduce_far), (2, self.reduce_near), (1, self.finish)])
+        self.run([(1, self.finish), (2, self.reduce_near), (7, self.feed), (5, self.reduce_far)])
         self.scatter()
         self.raster()
         for copy in (self.near, self.far, self.share):

time: 149 us -> 145 us (0.973)
  Pallas kernels: 147 us -> 143 us
    pallas_call x2, Pallas kernels: 147 us -> 143 us  [run_layer(): pl.pallas_call(kernel, out_shape=tuple(outputs.values()), in_specs=[place...]
where the time goes in v4:
time: 145 us
  Pallas kernels  143 us (99%)
  local copies, waits for them, and re-layouts  1.67 us (1%)
    pallas_call x2, Pallas kernels, run_layer(): pl.pallas_call(kernel, out_shape=tuple(outputs.values()), in_specs=[place...  143 us

profile of v4, /device:TPU:0, one launch (start us, length us, event | category | flops | bytes accessed | tf_op | source)
XLA Modules:
  0.0 145.0 jit_solution(2296865167139867676)
XLA Ops:
  0.0 64.7 %first.1 = (f32[1024,128]{1,0:T(8,128)}, s32[1,128]{1,0:T(1,128)}, s32[1,128]{1,0:T(1,128)}) custom-call(f32[1024,128]{1,0:T(8,128)} %refs_0_.1, s32[1,16]{1,0:T(1,128)} %bitcast.8, s32[1,16]{1,0:T(1,128)} %bitcast.9, f32[2,512]{1,0:T(2,128)} %refs_7_.3, f32[2,512]{1,0:T(2,128)} %refs_8_.3, f32[2,3,512,128]{3,2,1,0:T(8,128)} %refs_9_.1, ...), custom_call_target="tpu_custom_call" | custom-call | tf_op jit(solution)/shard_map/first/pallas_call | solution.py:1130
  64.7 78.6 %second.1 = f32[8,16,512]{2,1,0:T(8,128)} custom-call(s32[1,128]{1,0:T(1,128)} %get-tuple-element.8.refs_0_, s32[1,128]{1,0:T(1,128)} %get-tuple-element.9.refs_1_, f32[16,64,128]{2,1,0:T(8,128)} %bitcast.5, s32[1,1024]{1,0:T(1,128)} %bitcast.7, f32[3,3,2,512]{3,2,1,0:T(2,128)} %bitcast.6, f32[2,512]{1,0:T(2,128)} %refs_5_.3, f32[2,512,1024]{2,1,0:T(8,128)} %refs_6_.3, ...), custom_call_target="tpu_custom_call" | custom-call | tf_op jit(solution)/shard_map/second/pallas_call | solution.py:1130
  143.4 1.7 %copy.15 = f32[8,16,512]{2,1,0:T(8,128)} copy(f32[8,16,512]{2,1,0:T(8,128)} %second.1) | data formatting | bytes 524288

commit v5 on v4

--- a/solution.py
+++ b/solution.py
@@ -555,9 +555,10 @@
 
 
 class Layer:
-    def __init__(self, layer, refs, heads, chunk, kinds):
+    def __init__(self, layer, refs, heads, chunk):
         self.__dict__.update(refs)
-        self.layer, self.heads, self.chunk, self.kinds = layer, heads, chunk, kinds
+        self.layer, self.heads, self.chunk = layer, heads, chunk
+        self.tag = "_sem" + str(layer)
         self.cols, self.reps, self.c, self.r = position()
         self.ntok, self.t = lax.axis_size("tok"), lax.axis_index("tok")
         self.me = self.c * self.reps + self.r
@@ -566,11 +567,12 @@
         self.rows, self.width = self.a_s.shape
         self.lanes = self.q_s.shape[-1] // 2
         self.n = self.rows // chunk
-        self.started = []
+        self.block = self.y_s.shape[1]
+        self.cap = self.o_s.shape[1]
 
     def sent(self, kind, i, src, dst, device):
-        k = self.kinds.index(kind)
-        return remote(src, dst, self.sem.at[k, 0, i], self.sem.at[k, 1, i], device)
+        sem = getattr(self, kind + self.tag)
+        return remote(src, dst, sem.at[0, i], sem.at[1, i], device)
 
     def load_weights(self):
         pairs = (
@@ -578,24 +580,28 @@
             (self.wu_ref, self.wu_f), (self.wd_ref, self.wd_f),
         )
         self.loads = [
-            pltpu.make_async_copy(src.at[self.layer], dst, self.wsem.at[j])
+            pltpu.make_async_copy(src.at[self.layer], dst.at[self.layer], self.wsem.at[self.layer, j])
             for j, (src, dst) in enumerate(pairs)
         ]
         for load in self.loads:
             load.start()
 
     def split_weights(self):
+        layer = self.layer
         self.loads[0].wait()
         for m in range(3):
-            self.wqkv_s[0, m], self.wqkv_s[1, m] = split(self.wqkv_f[m])
+            self.wqkv_s[layer, 0, m], self.wqkv_s[layer, 1, m] = split(self.wqkv_f[layer, m])
         rest = ((self.wo_f, self.wo_s), (self.wu_f, self.wu_s), (self.wd_f, self.wd_s))
         for load, (src, dst) in zip(self.loads[1:], rest):
             load.wait()
-            dst[0], dst[1] = split(src[...])
+            dst[layer, 0], dst[layer, 1] = split(src[layer])
+
+    def pair(self, ref):
+        return ref[self.layer, 0], ref[self.layer, 1]
 
     def project(self, stream):
         normed = split(layer_norm(stream, self.ga_ref[pl.ds(self.layer, 1)]))
-        return [dot3(normed, (self.wqkv_s[0, m], self.wqkv_s[1, m])) for m in range(3)]
+        return [dot3(normed, (self.wqkv_s[self.layer, 0, m], self.wqkv_s[self.layer, 1, m])) for m in range(3)]
 
     def pack(self, at, q, k, v):
         lanes = self.lanes
@@ -667,7 +673,7 @@
         self.att_s[half] = total
 
     def finish(self, i):
-        projection = (self.wo_s[0], self.wo_s[1])
+        projection = self.pair(self.wo_s)
         self.p_s[piece(i, self.chunk)] = dot3(split(self.att_s[0] + self.att_s[1]), projection)
         self.near(i).start()
 
@@ -687,8 +693,8 @@
 
     def mlp(self, x):
         normed = split(layer_norm(x, self.gm_ref[pl.ds(self.layer, 1)]))
-        hidden = gelu(dot3(normed, (self.wu_s[0], self.wu_s[1])))
-        return dot3(split(hidden), (self.wd_s[0], self.wd_s[1]))
+        hidden = gelu(dot3(normed, self.pair(self.wu_s)))
+        return dot3(split(hidden), self.pair(self.wd_s))
 
     def run(self, stages):
         n = self.n
@@ -711,20 +717,20 @@
 class First(Layer):
     def stream_rows(self, start, count):
         at = pl.ds(pl.multiple_of(start, count), count)
-        return jnp.concatenate([self.g_s[j, at] for j in range(self.cols * self.reps)], axis=-1)
+        return jnp.concatenate([self.g0_s[j, at] for j in range(self.cols * self.reps)], axis=-1)
 
     def across(self, i):
         at = piece(i, self.chunk)
-        return self.sent("across", i, self.x_ref.at[at], self.g_s.at[self.me, at], self.peer)
+        return self.sent("across", i, self.tokens_ref.at[at], self.g0_s.at[self.me, at], self.peer)
 
     def over(self, i):
         at = piece(i, self.chunk)
-        return self.sent("over", i, self.x_ref.at[at], self.g_s.at[self.me, at], self.mate)
+        return self.sent("over", i, self.tokens_ref.at[at], self.g0_s.at[self.me, at], self.mate)
 
     def relay(self, i):
         at = piece(i, self.chunk)
         slot = (1 - self.c) * self.reps + self.r
-        return self.sent("relay", i, self.g_s.at[slot, at], self.g_s.at[slot, at], self.mate)
+        return self.sent("relay", i, self.g0_s.at[slot, at], self.g0_s.at[slot, at], self.mate)
 
     def code(self, e):
         target = {"tok": lax.rem(self.t + e, self.ntok)}
@@ -747,7 +753,7 @@
         block = lax.broadcasted_iota(jnp.int32, (count, 128), 0).astype(jnp.float32)
         index = jnp.sum(jnp.where(place == at, block, 0.0), axis=0, keepdims=True)
         code = jnp.sum(jnp.where(place == at, slots + 1.0, 0.0), axis=0, keepdims=True)
-        self.index_ref[...] = index.astype(jnp.int32)
+        self.index_v[...] = index.astype(jnp.int32)
         self.code_s[...] = jnp.broadcast_to(code, self.code_s.shape)
         self.arrived_s[self.t] = jnp.broadcast_to(code, self.code_s.shape)
 
@@ -763,7 +769,7 @@
             found = valid & (upright == (col + 1).astype(jnp.float32))
             entry = (row - first + u * self.cap).astype(jnp.float32)
             source += jnp.sum(jnp.where(found, entry, 0.0), axis=0, keepdims=True)
-        self.source_ref[...] = source.astype(jnp.int32)
+        self.source_v[...] = source.astype(jnp.int32)
 
     def near2(self, i):
         at = piece(i, self.chunk)
@@ -792,22 +798,27 @@
         at = piece(i, self.chunk)
         own = self.a_s[at, piece(self.me, self.lanes)]
         total = (self.m_s[self.r, self.c, at] + self.n2_s[self.c, at]) + self.f2_s[at]
-        self.out_ref[at] = total + own
-
-    def body(self):
+        count = self.chunk // self.block
+        self.y_s[piece(i, count)] = (total + own).reshape(count, self.block, self.lanes)
+
+    def body(self, second):
         n = self.n
-        self.load_weights()
-        greet([self.mate, self.peer] + self.peers)
         for i in range(n):
             self.across(i).start()
         for i in range(n):
             self.over(i).start()
-        self.cap = capacity_of(self.dd_ref.shape[1], self.ntok)
+        keep = pltpu.make_async_copy(self.tokens_ref, self.g0_s.at[self.me], self.tsem.at[0])
+        keep.start()
         self.route()
-        self.g_s[self.me] = self.x_ref[...]
+        table = pltpu.make_async_copy(self.index_v, self.index_m, self.tsem.at[1])
+        table.start()
         self.split_weights()
         for e in range(1, self.ntok):
             self.code(e).start()
+        second.split_weights()
+        second.split_points()
+        keep.wait()
+        table.wait()
 
         def step(i, carry):
             @pl.when(i < n)
@@ -839,13 +850,22 @@
         for e in range(1, self.ntok):
             self.code(e).wait()
         self.locate()
+        table = pltpu.make_async_copy(self.source_v, self.source_m, self.tsem.at[2])
+        table.start()
+        table.wait()
 
 
 class Second(Layer):
+    def entry(self, k):
+        return jnp.clip(self.source_m[0, k], 0, self.ntok * self.cap - 1)
+
+    def chosen(self, u, j):
+        return jnp.clip(self.index_m[0, u * self.cap + j], 0, self.y_s.shape[0] - 1)
+
     def stream_rows(self, start, count):
         parts = []
         for m in range(count // self.block):
-            at = self.source_ref[0, start // self.block + m]
+            at = self.entry(start // self.block + m)
             places = [self.g_s[at // self.cap, j, at % self.cap] for j in range(self.cols * self.reps)]
             parts.append(jnp.concatenate(places, axis=-1))
         return jnp.concatenate(parts, axis=0)
@@ -902,20 +922,17 @@
             self.order += [e] + ([self.ntok - e] if self.ntok - e != e else [])
         for u in range(self.ntok):
             for j in range(self.cap):
-                self.o_s[u, j] = self.x_ref[self.index_ref[0, u * self.cap + j]]
+                self.o_s[u, j] = self.y_s[self.chosen(u, j)]
         for j in range(self.cap):
-            self.g_s[self.t, self.me, j] = self.x_ref[self.index_ref[0, self.t * self.cap + j]]
+            self.g_s[self.t, self.me, j] = self.y_s[self.chosen(self.t, j)]
         for j in range(self.cap):
             for e in self.order[1:]:
                 self.along(e, j).start()
         for j in range(self.cap):
             self.across(0, j).start()
             self.over(0, j).start()
-        self.split_weights()
         for j in range(self.cap):
             self.arrive(j)
-            if j == 0:
-                self.split_points()
             if j >= 1:
                 self.hand(j - 1)
             if j >= 2:
@@ -927,7 +944,7 @@
         def step(i, carry):
             def row(m):
                 each = self.chunk // self.block
-                blocks = [self.raw_s[m, self.source_ref[0, i * each + k]] for k in range(each)]
+                blocks = [self.raw_s[m, self.entry(i * each + k)] for k in range(each)]
                 return jnp.concatenate(blocks, axis=0)
 
             self.pack(piece(i, self.chunk), row(0), row(1), row(2))
@@ -936,7 +953,7 @@
         lax.fori_loop(0, self.n, step, 0)
 
     def load_points(self):
-        self.point = pltpu.make_async_copy(self.pw_ref, self.pw_f, self.wsem.at[4])
+        self.point = pltpu.make_async_copy(self.pw_ref, self.pw_f, self.tsem.at[3])
         self.point.start()
 
     def split_points(self):
@@ -1054,14 +1071,7 @@
             self.out_ref[y] = self.tile_s[pl.ds((y + HALO) * wide + HALO, TC)]
 
     def body(self):
-        self.block = self.x_ref.shape[1]
-        self.cap = self.g_s.shape[2]
         self.pieces, self.edge = self.s3_s.shape[:2]
-        step = jnp.where(self.r == 0, self.ntok - 1, 1)
-        self.partner = {"tok": lax.rem(self.t + step, self.ntok), "rep": 1 - self.r}
-        self.load_weights()
-        self.load_points()
-        greet([self.mate, self.peer, self.partner] + self.peers)
         self.move()
         self.pool_s[...] = jnp.zeros(self.pool_s.shape, jnp.float32)
         self.run([(1, self.finish), (2, self.reduce_near), (7, self.feed), (5, self.reduce_far)])
@@ -1082,120 +1092,87 @@
             self.far3(k).wait_send()
 
 
-def run_layer(kind, layer, inputs, outputs, weights, collective_id, extra, kinds, most):
+def capacity_of(count, peers):
+    return max(2, (count + peers - 4) // (peers - 1))
+
+
+def both_layers(tokens, dest_device, dest_slot, cap, pillar, raster_weights, weights, collective_id):
     w_qkv, w_out, w_up, w_down, attn_gain, mlp_gain = weights
-    lanes, width, hidden = w_qkv.shape[-1], w_qkv.shape[-2], w_up.shape[-1]
-    heads, rows = lanes // HD, PATCH
-    chunk = min(256, rows)
+    depth_weight, point_weight, raster_gain = raster_weights
+    cols, reps, ntok = lax.axis_size("col"), lax.axis_size("rep"), lax.axis_size("tok")
+    rows, lanes = tokens.shape
+    width, hidden, count = w_qkv.shape[-2], w_up.shape[-1], dest_device.shape[0]
+    block, heads, chunk = rows // count, lanes // HD, min(256, rows)
+    n = rows // chunk
+    wide, rep_rows = TC + 2 * HALO, TR // reps
+    edge, pieces = HALO * wide, rep_rows // HALO
+    tile = (rep_rows + 2 * HALO) * wide
     dma, f32, b16 = pltpu.SemaphoreType.DMA, jnp.float32, jnp.bfloat16
-    vmem = pl.BlockSpec(memory_space=pltpu.VMEM)
-    hbm = pl.BlockSpec(memory_space=pl.ANY)
-    smem = pl.BlockSpec(memory_space=pltpu.SMEM)
-    inputs = dict(inputs)
-    places = {name: vmem for name in inputs}
-    inputs.update(ga_ref=attn_gain, gm_ref=mlp_gain)
-    inputs.update(wqkv_ref=w_qkv, wo_ref=w_out, wu_ref=w_up, wd_ref=w_down)
-    for name in ("index_ref", "source_ref"):
-        if name in inputs:
-            places[name] = smem
-    for name in ("wqkv_ref", "wo_ref", "wu_ref", "wd_ref", "pw_ref"):
-        places[name] = hbm
-    scratch = dict(
-        wqkv_f=pltpu.VMEM((3, width, lanes), f32),
-        wo_f=pltpu.VMEM((lanes, width), f32),
-        wu_f=pltpu.VMEM((width, hidden), f32),
-        wd_f=pltpu.VMEM((hidden, width), f32),
-        wqkv_s=pltpu.VMEM((2, 3, width, lanes), b16),
-        wo_s=pltpu.VMEM((2, lanes, width), b16),
-        wu_s=pltpu.VMEM((2, width, hidden), b16),
-        wd_s=pltpu.VMEM((2, hidden, width), b16),
-        q_s=pltpu.VMEM((2, rows, 2 * lanes), b16),
-        k_s=pltpu.VMEM((2, rows, 2 * lanes), b16),
-        v_s=pltpu.VMEM((2, rows, 2 * lanes), b16),
-        att_s=pltpu.VMEM((2, chunk, lanes), f32),
-        p_s=pltpu.VMEM((rows, width), f32),
-        n1_s=pltpu.VMEM((rows // 2, width), f32),
-        s1_s=pltpu.VMEM((rows // 2, width), f32),
-        f1_s=pltpu.VMEM((rows // 2, width), f32),
-        a_s=pltpu.VMEM((rows, width), f32),
-        sem=dma((len(kinds), 2, max(most, rows // chunk))),
-        wsem=dma((5,)),
+    places = {True: pl.BlockSpec(memory_space=pltpu.VMEM), False: pl.BlockSpec(memory_space=pl.ANY)}
+    inputs = dict(
+        tokens_ref=tokens, wqkv_ref=w_qkv, wo_ref=w_out, wu_ref=w_up, wd_ref=w_down, pw_ref=point_weight,
+        ga_ref=attn_gain, gm_ref=mlp_gain, dd_ref=dest_device[None, :], ds_ref=dest_slot[None, :],
+        pillar_ref=pillar[None, :], dw_ref=jnp.transpose(depth_weight, (1, 2, 0, 3)), rg_ref=raster_gain,
     )
-    scratch.update(extra)
-    names = list(inputs) + list(outputs) + list(scratch)
+    far_away = ("tokens_ref", "wqkv_ref", "wo_ref", "wu_ref", "wd_ref", "pw_ref")
+    floats = dict(
+        wqkv_f=(2, 3, width, lanes), wo_f=(2, lanes, width), wu_f=(2, width, hidden),
+        wd_f=(2, hidden, width), att_s=(2, chunk, lanes), p_s=(rows, width), n1_s=(rows // 2, width),
+        s1_s=(rows // 2, width), f1_s=(rows // 2, width), a_s=(rows, width),
+        g0_s=(cols * reps, rows, lanes), m_s=(reps, cols, rows, lanes), n2_s=(cols, rows, lanes),
+        s2_s=(rows, lanes), f2_s=(rows, lanes), code_s=(8, 128), arrived_s=(ntok, 8, 128),
+        y_s=(count, block, lanes), o_s=(ntok, cap, block, lanes),
+        g_s=(ntok, cols * reps, cap, block, lanes), raw_s=(3, ntok * cap, block, lanes),
+        pw_f=point_weight.shape, pool_s=(cols * reps * rep_rows * wide, width),
+        n3_s=(2, pieces, edge, width), s3_s=(pieces, edge, width), f3_s=(pieces, edge, width),
+        h_s=(2, edge, width), tile_s=(tile, width), flat_s=(tile + 16, width),
+    )
+    halves = dict(
+        wqkv_s=(2, 2, 3, width, lanes), wo_s=(2, 2, lanes, width), wu_s=(2, 2, width, hidden),
+        wd_s=(2, 2, hidden, width), q_s=(2, rows, 2 * lanes), k_s=(2, rows, 2 * lanes),
+        v_s=(2, rows, 2 * lanes), pw_s=(2,) + point_weight.shape,
+    )
+    scratch = {name: pltpu.VMEM(shape, f32) for name, shape in floats.items()}
+    scratch.update({name: pltpu.VMEM(shape, b16) for name, shape in halves.items()})
+    for name in ("index", "source"):
+        scratch[name + "_v"] = pltpu.VMEM((1, 128), jnp.int32)
+        scratch[name + "_m"] = pltpu.SMEM((1, 128), jnp.int32)
+    for kind in ("near", "far", "share", "near2", "far2", "across", "over", "relay"):
+        scratch[kind + "_sem0"] = dma((2, n))
+    scratch["code_sem0"] = dma((2, ntok))
+    for kind in ("near", "far", "share"):
+        scratch[kind + "_sem1"] = dma((2, n))
+    for kind in ("along", "across", "over", "relay"):
+        scratch[kind + "_sem1"] = dma((2, ntok * cap))
+    scratch["near3_sem1"] = dma((2, 2 * pieces))
+    scratch["far3_sem1"] = dma((2, pieces))
+    scratch["halo_sem1"] = dma((2, 2))
+    scratch["wsem"], scratch["tsem"] = dma((2, 4)), dma((4,))
+    names = list(inputs) + ["out_ref"] + list(scratch)
 
     def kernel(*refs):
-        kind(layer, dict(zip(names, refs)), heads, chunk, kinds).body()
+        refs = dict(zip(names, refs))
+        first, second = First(0, refs, heads, chunk), Second(1, refs, heads, chunk)
+        step = jnp.where(first.r == 0, ntok - 1, 1)
+        second.partner = {"tok": lax.rem(first.t + step, ntok), "rep": 1 - first.r}
+        first.load_weights()
+        second.load_weights()
+        second.load_points()
+        greet([first.mate, first.peer, second.partner] + first.peers)
+        first.body(second)
+        second.body()
 
     return pl.pallas_call(
         kernel,
-        out_shape=tuple(outputs.values()),
-        in_specs=[places.get(name, vmem) for name in inputs],
-        out_specs=tuple(vmem for _ in outputs),
+        out_shape=jax.ShapeDtypeStruct((rep_rows, TC, width), f32),
+        in_specs=[places[name not in far_away] for name in inputs],
+        out_specs=places[True],
         scratch_shapes=list(scratch.values()),
         compiler_params=pltpu.CompilerParams(
             collective_id=collective_id, has_side_effects=True, vmem_limit_bytes=VMEM_LIMIT
         ),
-        name=kind.__name__.lower(),
+        name="layers",
     )(*inputs.values())
-
-
-def capacity_of(count, peers):
-    return max(2, (count + peers - 4) // (peers - 1))
-
-
-def first_layer(tokens, dest_device, dest_slot, weights, collective_id):
-    rows, lanes = tokens.shape
-    cols, reps, ntok = lax.axis_size("col"), lax.axis_size("rep"), lax.axis_size("tok")
-    f32 = jnp.float32
-    extra = dict(
-        g_s=pltpu.VMEM((cols * reps, rows, lanes), f32),
-        m_s=pltpu.VMEM((reps, cols, rows, lanes), f32),
-        n2_s=pltpu.VMEM((cols, rows, lanes), f32),
-        s2_s=pltpu.VMEM((rows, lanes), f32),
-        f2_s=pltpu.VMEM((rows, lanes), f32),
-        code_s=pltpu.VMEM((8, 128), f32),
-        arrived_s=pltpu.VMEM((ntok, 8, 128), f32),
-    )
-    kinds = ("near", "far", "share", "near2", "far2", "across", "over", "relay", "code")
-    table = jax.ShapeDtypeStruct((1, 128), jnp.int32)
-    outputs = dict(
-        out_ref=jax.ShapeDtypeStruct((rows, lanes), f32), index_ref=table, source_ref=table
-    )
-    inputs = dict(x_ref=tokens, dd_ref=dest_device[None, :], ds_ref=dest_slot[None, :])
-    return run_layer(First, 0, inputs, outputs, weights, collective_id, extra, kinds, ntok)
-
-
-def second_layer(share, index, source, cap, pillar, raster_weights, weights, collective_id):
-    cols, reps, ntok = lax.axis_size("col"), lax.axis_size("rep"), lax.axis_size("tok")
-    count, block, lanes = share.shape
-    depth_weight, point_weight, raster_gain = raster_weights
-    width = depth_weight.shape[-1]
-    wide, rep_rows = TC + 2 * HALO, TR // reps
-    edge, pieces = HALO * wide, rep_rows // HALO
-    tile = (rep_rows + 2 * HALO) * wide
-    f32 = jnp.float32
-    extra = dict(
-        o_s=pltpu.VMEM((ntok, cap, block, lanes), f32),
-        g_s=pltpu.VMEM((ntok, cols * reps, cap, block, lanes), f32),
-        raw_s=pltpu.VMEM((3, ntok * cap, block, lanes), f32),
-        pw_f=pltpu.VMEM(point_weight.shape, f32),
-        pw_s=pltpu.VMEM((2,) + point_weight.shape, jnp.bfloat16),
-        pool_s=pltpu.VMEM((cols * reps * rep_rows * wide, width), f32),
-        n3_s=pltpu.VMEM((2, pieces, edge, width), f32),
-        s3_s=pltpu.VMEM((pieces, edge, width), f32),
-        f3_s=pltpu.VMEM((pieces, edge, width), f32),
-        h_s=pltpu.VMEM((2, edge, width), f32),
-        tile_s=pltpu.VMEM((tile, width), f32),
-        flat_s=pltpu.VMEM((tile + 16, width), f32),
-    )
-    kinds = ("near", "far", "share", "along", "across", "over", "relay", "near3", "far3", "halo")
-    outputs = dict(out_ref=jax.ShapeDtypeStruct((rep_rows, TC, width), f32))
-    inputs = dict(
-        index_ref=index, source_ref=source, x_ref=share, pillar_ref=pillar[None, :],
-        dw_ref=jnp.transpose(depth_weight, (1, 2, 0, 3)), rg_ref=raster_gain, pw_ref=point_weight,
-    )
-    return run_layer(Second, 1, inputs, outputs, weights, collective_id, extra, kinds, ntok * cap)[0]
 
 
 HALO = 2
@@ -1295,10 +1272,8 @@
     weights = (w_qkv, w_out, w_up, w_down, attn_gain, mlp_gain)
     whole = (2 * members[1] * HALO * (TC + 2 * HALO)) % 8 == 0 and TR % (members[1] * HALO) == 0
     if members == (2, 2) and ntok > 1 and tokens.shape[0] == PATCH and whole and ntok * capacity <= 128:
-        share, index, source = first_layer(tokens, dest_device, dest_slot, weights, 1)
-        share = share.reshape(block_count, -1, width)
         raster_weights = (depth_weight, point_weight, raster_gain)
-        return second_layer(share, index, source, capacity, pillar, raster_weights, weights, 5)
+        return both_layers(tokens, dest_device, dest_slot, capacity, pillar, raster_weights, weights, 1)
     blocks = gather(tokens, 1).reshape(1, group, block_count, -1, width)
     stream = attention_layer(blocks, order, 0, w_qkv, w_out, attn_gain, 2)
     share = scatter(mlp_partial(stream, 0, w_up, w_down, mlp_gain, group), 3)

time: 145 us -> 140 us (0.966)
  Pallas kernels: 143 us -> 138 us
    pallas_call x2 -> x1, Pallas kernels: 143 us -> 138 us  [both_layers(): pl.pallas_call(kernel, out_shape=jax.ShapeDtypeStruct((rep_rows, TC, widt...]
where the time goes in v5:
time: 140 us
  Pallas kernels  138 us (99%)
  local copies, waits for them, and re-layouts  1.67 us (1%)
    pallas_call x1, Pallas kernels, both_layers(): pl.pallas_call(kernel, out_shape=jax.ShapeDtypeStruct((rep_rows, TC, widt...  138 us

profile of v5, /device:TPU:0, one launch (start us, length us, event | category | flops | bytes accessed | tf_op | source)
XLA Modules:
  0.0 139.9 jit_solution(11083474143727042591)
XLA Ops:
  0.0 138.2 %layers.1 = f32[8,16,512]{2,1,0:T(8,128)} custom-call(f32[1024,128]{1,0:T(8,128)} %refs_0_.1, f32[2,3,512,128]{3,2,1,0:T(8,128)} %refs_1_.1, f32[2,128,512]{2,1,0:T(8,128)} %refs_2_.1, f32[2,512,512]{2,1,0:T(8,128)} %refs_3_.1, f32[2,512,512]{2,1,0:T(8,128)} %refs_4_.1, f32[2,512,1024]{2,1,0:T(8,128)} %refs_5_.1, f32[2,512]{1,0:T(2,128)} %refs_6_.1, ...), custom_call_target="tpu_custom_call" | custom-call | tf_op jit(solution)/shard_map/layers/pallas_call | solution.py:1165
  138.2 1.7 %copy.15 = f32[8,16,512]{2,1,0:T(8,128)} copy(f32[8,16,512]{2,1,0:T(8,128)} %layers.1) | data formatting | bytes 524288

commit v6 on v5

--- a/solution.py
+++ b/solution.py
@@ -817,6 +817,7 @@
             self.code(e).start()
         second.split_weights()
         second.split_points()
+        self.pool_s[...] = jnp.zeros(self.pool_s.shape, jnp.float32)
         keep.wait()
         table.wait()
 
@@ -847,12 +848,14 @@
         ):
             for i in range(n):
                 copy(i).wait_send()
+
+    def tables(self):
         for e in range(1, self.ntok):
             self.code(e).wait()
         self.locate()
         table = pltpu.make_async_copy(self.source_v, self.source_m, self.tsem.at[2])
         table.start()
-        table.wait()
+        return table
 
 
 class Second(Layer):
@@ -916,30 +919,30 @@
                 entry = self.origin(e) * self.cap + j
                 self.raw_s[m, entry] = values[at * self.block : (at + 1) * self.block]
 
-    def move(self):
+    def move(self, first):
         self.order = [0]
         for e in range(1, self.ntok // 2 + 1):
             self.order += [e] + ([self.ntok - e] if self.ntok - e != e else [])
-        for u in range(self.ntok):
-            for j in range(self.cap):
+        for j in range(self.cap):
+            for u in range(self.ntok):
                 self.o_s[u, j] = self.y_s[self.chosen(u, j)]
-        for j in range(self.cap):
-            self.g_s[self.t, self.me, j] = self.y_s[self.chosen(self.t, j)]
-        for j in range(self.cap):
             for e in self.order[1:]:
                 self.along(e, j).start()
         for j in range(self.cap):
+            self.g_s[self.t, self.me, j] = self.y_s[self.chosen(self.t, j)]
             self.across(0, j).start()
             self.over(0, j).start()
+        table = first.tables()
         for j in range(self.cap):
             self.arrive(j)
             if j >= 1:
                 self.hand(j - 1)
             if j >= 2:
                 self.take(j - 2)
+        self.take(self.cap - 2)
         self.hand(self.cap - 1)
-        for j in range(max(0, self.cap - 2), self.cap):
-            self.take(j)
+        self.take(self.cap - 1)
+        table.wait()
 
         def step(i, carry):
             def row(m):
@@ -1070,10 +1073,9 @@
         for y in range(rows - 2 * HALO):
             self.out_ref[y] = self.tile_s[pl.ds((y + HALO) * wide + HALO, TC)]
 
-    def body(self):
+    def body(self, first):
         self.pieces, self.edge = self.s3_s.shape[:2]
-        self.move()
-        self.pool_s[...] = jnp.zeros(self.pool_s.shape, jnp.float32)
+        self.move(first)
         self.run([(1, self.finish), (2, self.reduce_near), (7, self.feed), (5, self.reduce_far)])
         self.scatter()
         self.raster()
@@ -1160,7 +1162,7 @@
         second.load_points()
         greet([first.mate, first.peer, second.partner] + first.peers)
         first.body(second)
-        second.body()
+        second.body(first)
 
     return pl.pallas_call(
         kernel,

time: 140 us -> 140 us (level)
  no operation moved by 1% of the time
where the time goes in v6:
time: 140 us
  Pallas kernels  138 us (99%)
  local copies, waits for them, and re-layouts  1.67 us (1%)
    pallas_call x1, Pallas kernels, both_layers(): pl.pallas_call(kernel, out_shape=jax.ShapeDtypeStruct((rep_rows, TC, widt...  138 us

profile of v6, /device:TPU:0, one launch (start us, length us, event | category | flops | bytes accessed | tf_op | source)
XLA Modules:
  0.0 139.5 jit_solution(5746474161568119927)
XLA Ops:
  0.0 137.9 %layers.1 = f32[8,16,512]{2,1,0:T(8,128)} custom-call(f32[1024,128]{1,0:T(8,128)} %refs_0_.1, f32[2,3,512,128]{3,2,1,0:T(8,128)} %refs_1_.1, f32[2,128,512]{2,1,0:T(8,128)} %refs_2_.1, f32[2,512,512]{2,1,0:T(8,128)} %refs_3_.1, f32[2,512,512]{2,1,0:T(8,128)} %refs_4_.1, f32[2,512,1024]{2,1,0:T(8,128)} %refs_5_.1, f32[2,512]{1,0:T(2,128)} %refs_6_.1, ...), custom_call_target="tpu_custom_call" | custom-call | tf_op jit(solution)/shard_map/layers/pallas_call | solution.py:1167
  137.9 1.7 %copy.15 = f32[8,16,512]{2,1,0:T(8,128)} copy(f32[8,16,512]{2,1,0:T(8,128)} %layers.1) | data formatting | bytes 524288

commit v7 on v6

--- a/solution.py
+++ b/solution.py
@@ -567,6 +567,7 @@
         self.rows, self.width = self.a_s.shape
         self.lanes = self.q_s.shape[-1] // 2
         self.n = self.rows // chunk
+        self.part = chunk // 2
         self.block = self.y_s.shape[1]
         self.cap = self.o_s.shape[1]
 
@@ -720,15 +721,15 @@
         return jnp.concatenate([self.g0_s[j, at] for j in range(self.cols * self.reps)], axis=-1)
 
     def across(self, i):
-        at = piece(i, self.chunk)
+        at = piece(i, self.part)
         return self.sent("across", i, self.tokens_ref.at[at], self.g0_s.at[self.me, at], self.peer)
 
     def over(self, i):
-        at = piece(i, self.chunk)
+        at = piece(i, self.part)
         return self.sent("over", i, self.tokens_ref.at[at], self.g0_s.at[self.me, at], self.mate)
 
     def relay(self, i):
-        at = piece(i, self.chunk)
+        at = piece(i, self.part)
         slot = (1 - self.c) * self.reps + self.r
         return self.sent("relay", i, self.g0_s.at[slot, at], self.g0_s.at[slot, at], self.mate)
 
@@ -802,7 +803,7 @@
         self.y_s[piece(i, count)] = (total + own).reshape(count, self.block, self.lanes)
 
     def body(self, second):
-        n = self.n
+        n = self.rows // self.part
         for i in range(n):
             self.across(i).start()
         for i in range(n):
@@ -831,21 +832,22 @@
             def _():
                 self.over(i - 1).wait_recv()
                 self.relay(i - 1).wait_recv()
-                stream = self.stream_rows((i - 1) * self.chunk, self.chunk)
-                self.pack(piece(i - 1, self.chunk), *self.project(stream))
+                stream = self.stream_rows((i - 1) * self.part, self.part)
+                self.pack(piece(i - 1, self.part), *self.project(stream))
 
             return carry
 
         lax.fori_loop(0, n + 1, step, 0)
         self.run(
             [
-                (1, self.finish), (2, self.reduce_near), (9, self.scatter_near),
-                (6, self.reduce_far), (7, self.feed), (13, self.scatter_far),
+                (1, self.finish), (2, self.reduce_near), (10, self.scatter_near),
+                (7, self.reduce_far), (8, self.feed), (15, self.scatter_far),
             ]
         )
-        for copy in (
-            self.near, self.far, self.share, self.near2, self.far2, self.across, self.over, self.relay
-        ):
+        for copy in (self.near, self.far, self.share, self.near2, self.far2):
+            for i in range(self.n):
+                copy(i).wait_send()
+        for copy in (self.across, self.over, self.relay):
             for i in range(n):
                 copy(i).wait_send()
 
@@ -1076,7 +1078,7 @@
     def body(self, first):
         self.pieces, self.edge = self.s3_s.shape[:2]
         self.move(first)
-        self.run([(1, self.finish), (2, self.reduce_near), (7, self.feed), (5, self.reduce_far)])
+        self.run([(1, self.finish), (2, self.reduce_near), (8, self.feed), (6, self.reduce_far)])
         self.scatter()
         self.raster()
         for copy in (self.near, self.far, self.share):
@@ -1139,8 +1141,10 @@
     for name in ("index", "source"):
         scratch[name + "_v"] = pltpu.VMEM((1, 128), jnp.int32)
         scratch[name + "_m"] = pltpu.SMEM((1, 128), jnp.int32)
-    for kind in ("near", "far", "share", "near2", "far2", "across", "over", "relay"):
+    for kind in ("near", "far", "share", "near2", "far2"):
         scratch[kind + "_sem0"] = dma((2, n))
+    for kind in ("across", "over", "relay"):
+        scratch[kind + "_sem0"] = dma((2, 2 * n))
     scratch["code_sem0"] = dma((2, ntok))
     for kind in ("near", "far", "share"):
         scratch[kind + "_sem1"] = dma((2, n))

time: 140 us -> 140 us (level)
  no operation moved by 1% of the time
where the time goes in v7:
time: 140 us
  Pallas kernels  138 us (99%)
  local copies, waits for them, and re-layouts  1.67 us (1%)
    pallas_call x1, Pallas kernels, both_layers(): pl.pallas_call(kernel, out_shape=jax.ShapeDtypeStruct((rep_rows, TC, widt...  138 us

profile of v7, /device:TPU:0, one launch (start us, length us, event | category | flops | bytes accessed | tf_op | source)
XLA Modules:
  0.0 139.7 jit_solution(11594045949634982722)
XLA Ops:
  0.0 138.0 %layers.1 = f32[8,16,512]{2,1,0:T(8,128)} custom-call(f32[1024,128]{1,0:T(8,128)} %refs_0_.1, f32[2,3,512,128]{3,2,1,0:T(8,128)} %refs_1_.1, f32[2,128,512]{2,1,0:T(8,128)} %refs_2_.1, f32[2,512,512]{2,1,0:T(8,128)} %refs_3_.1, f32[2,512,512]{2,1,0:T(8,128)} %refs_4_.1, f32[2,512,1024]{2,1,0:T(8,128)} %refs_5_.1, f32[2,512]{1,0:T(2,128)} %refs_6_.1, ...), custom_call_target="tpu_custom_call" | custom-call | tf_op jit(solution)/shard_map/layers/pallas_call | solution.py:1171
  138.0 1.7 %copy.15 = f32[8,16,512]{2,1,0:T(8,128)} copy(f32[8,16,512]{2,1,0:T(8,128)} %layers.1) | data formatting | bytes 524288

commit v8 on v6

--- a/solution.py
+++ b/solution.py
@@ -817,6 +817,7 @@
             self.code(e).start()
         second.split_weights()
         second.split_points()
+        second.choose()
         self.pool_s[...] = jnp.zeros(self.pool_s.shape, jnp.float32)
         keep.wait()
         table.wait()
@@ -986,8 +987,13 @@
         at = piece(i, self.chunk)
         x = self.a_s[at]
         high, low = split(self.mlp(x) + x * (1.0 / (self.cols * self.reps)))
-        chosen = jnp.where(self.cell_ids() == self.pillar_ref[:, at], 1.0, 0.0).astype(jnp.bfloat16)
+        chosen = self.hot_s[i]
         self.pool_s[...] += bdot(chosen, high) + bdot(chosen, low)
+
+    def choose(self):
+        for i in range(self.n):
+            pillar = self.pillar_ref[:, i * self.chunk : (i + 1) * self.chunk]
+            self.hot_s[i] = jnp.where(self.cell_ids() == pillar, 1.0, 0.0).astype(jnp.bfloat16)
 
     def tile_part(self, c, r, k):
         cells = self.pool_s.shape[0] // (self.cols * self.reps)
@@ -1133,6 +1139,7 @@
         wqkv_s=(2, 2, 3, width, lanes), wo_s=(2, 2, lanes, width), wu_s=(2, 2, width, hidden),
         wd_s=(2, 2, hidden, width), q_s=(2, rows, 2 * lanes), k_s=(2, rows, 2 * lanes),
         v_s=(2, rows, 2 * lanes), pw_s=(2,) + point_weight.shape,
+        hot_s=(n, cols * reps * rep_rows * wide, chunk),
     )
     scratch = {name: pltpu.VMEM(shape, f32) for name, shape in floats.items()}
     scratch.update({name: pltpu.VMEM(shape, b16) for name, shape in halves.items()})

time: 140 us -> 139 us (level)
  no operation moved by 1% of the time
where the time goes in v8:
time: 139 us
  Pallas kernels  138 us (99%)
  local copies, waits for them, and re-layouts  1.67 us (1%)
    pallas_call x1, Pallas kernels, both_layers(): pl.pallas_call(kernel, out_shape=jax.ShapeDtypeStruct((rep_rows, TC, widt...  138 us

profile of v8, /device:TPU:0, one launch (start us, length us, event | category | flops | bytes accessed | tf_op | source)
XLA Modules:
  0.0 139.3 jit_solution(10978693036661259343)
XLA Ops:
  0.0 137.6 %layers.1 = f32[8,16,512]{2,1,0:T(8,128)} custom-call(f32[1024,128]{1,0:T(8,128)} %refs_0_.1, f32[2,3,512,128]{3,2,1,0:T(8,128)} %refs_1_.1, f32[2,128,512]{2,1,0:T(8,128)} %refs_2_.1, f32[2,512,512]{2,1,0:T(8,128)} %refs_3_.1, f32[2,512,512]{2,1,0:T(8,128)} %refs_4_.1, f32[2,512,1024]{2,1,0:T(8,128)} %refs_5_.1, f32[2,512]{1,0:T(2,128)} %refs_6_.1, ...), custom_call_target="tpu_custom_call" | custom-call | tf_op jit(solution)/shard_map/layers/pallas_call | solution.py:1174
  137.6 1.7 %copy.15 = f32[8,16,512]{2,1,0:T(8,128)} copy(f32[8,16,512]{2,1,0:T(8,128)} %layers.1) | data formatting | bytes 524288
